TPU v7x, 128 devices: a whole 4x4x4 slice. The times are simulated.
128 devices in a mesh: frames: 32 (over y, x, core), expert: 4 (over z).
Axes of the slice: x: 4, y: 4, z: 4, core: 2. Of those that a mesh axis runs over, the one named last changes fastest.
Arguments:
- residual: bfloat16 [32, 512, 1152], P('frames', 'expert'), may hold values from -6 to 6
- queries: bfloat16 [32, 512, 1152], P('frames', 'expert'), may hold values from -8 to 8
- keys_in: bfloat16 [32, 512, 1152], P('frames', 'expert'), may hold values from -8 to 8
- values: bfloat16 [32, 512, 1152], P('frames', 'expert'), may hold values from -6 to 6
- w_out: bfloat16 [1152, 1152], replicated, may hold values from -0.1875 to 0.1875
- norm_gain: float32 [1152], replicated, may hold values from 0.5 to 2
- w_router: bfloat16 [1152, 64], replicated, may hold values from -0.1875 to 0.1875
- routes: int32 [4, 32, 128, 2], P('expert', 'frames'), may hold values from 0 to 63, all different within a row; in each aligned block of 128 rows (0 to 127, 128 to 255, ..., all dimensions but the last counted through in order) at most 8 rows name the same one
- w_gate: bfloat16 [128, 1152, 512], P(('frames', 'expert')), may hold values from -0.1875 to 0.1875
- w_up: bfloat16 [128, 1152, 512], P(('frames', 'expert')), may hold values from -0.1875 to 0.1875
- w_down: bfloat16 [128, 512, 1152], P(('frames', 'expert')), may hold values from -0.1875 to 0.1875
- d_out: bfloat16 [32, 512, 1152], P('frames', 'expert'), may hold values from -2 to 2
Outputs:
- block_out: bfloat16 [32, 512, 1152], P('frames', 'expert')
- d_hidden: bfloat16 [32, 512, 1152], P('frames', 'expert')
- d_gate: float32 [128, 1152, 512], P(('frames', 'expert'))
- d_up: float32 [128, 1152, 512], P(('frames', 'expert'))
- d_down: float32 [128, 512, 1152], P(('frames', 'expert'))
Inputs may be any that keep to these rules, and one draw needn't show every extreme that they name: `routes`: the two experts of a token differ. In the rows of one device (the aligned blocks of 128 rows over the flattened leading dimensions) no expert is named more than 8 times; some expert is named exactly 8 times in some of these blocks.
All inputs are finite; a program needn't handle non-finite values.
Results may differ from a plain program's by a relative error of at most 0.018.
Values may be sent and summed in bfloat16 or wider, within the bound.
No kernel may reach another device: no remote copies, remote signals or barrier semaphores. Data moves between devices by JAX's collectives and lax.ppermute only.
A program may use at most 128 MiB of HBM per device.

v0:
```python
import jax
import jax.numpy as jnp
from jax import lax
from jax.experimental import pallas as pl
from jax.experimental.pallas import tpu as pltpu
from jax.sharding import PartitionSpec as P

H = 16
F32 = jnp.float32
BF16 = jnp.bfloat16
WIDE = 640
STEP = 512
LIMIT = 48 * 1024 * 1024


def call(body, outs, cost, **extra):
    flops, moved = cost
    return pl.pallas_call(
        body,
        out_shape=outs,
        compiler_params=pltpu.CompilerParams(vmem_limit_bytes=LIMIT),
        cost_estimate=pl.CostEstimate(flops=flops, bytes_accessed=moved, transcendentals=0),
        **extra,
    )


def shape(dims, dtype):
    return jax.ShapeDtypeStruct(dims, dtype)


def rows_of(blocks):
    n, eight, width = blocks.shape
    return blocks.astype(F32).reshape(n * eight, width)


def blocks_of(rows):
    total, width = rows.shape
    return rows.reshape(total // 8, 8, width).astype(BF16)


def pack_body(q_ref, k_ref, v_ref, out_ref):
    for s, ref in enumerate((q_ref, k_ref, v_ref)):
        for i in range(ref.shape[0] // 8):
            for half in range(2):
                out_ref[2 * i + half, 8 * s : 8 * s + 8, :] = ref[
                    8 * i : 8 * i + 8, STEP * half : STEP * half + WIDE
                ]


def pair_onehots(routes_ref, experts):
    tok = routes_ref.shape[0]
    lanes = lax.broadcasted_iota(jnp.int32, (tok, experts), 1)
    return [routes_ref[:, j : j + 1] == lanes for j in range(2)]


def to_slots(picks, rows, out_ref):
    slots = picks.shape[1]
    step = 128
    for at in range(0, slots, step):
        moved = lax.dot_general(
            picks[:, at : at + step], rows, (((0,), (0,)), ((), ())), preferred_element_type=F32
        )
        blocks = blocks_of(moved)
        out_ref[at // 8 : (at + step) // 8, 0] = blocks
        out_ref[at // 8 : (at + step) // 8, 1] = blocks


def route_body(experts, routes_ref, cot_ref, pick0_ref, pick1_ref, out_ref):
    tok = routes_ref.shape[0]
    slots = pick0_ref.shape[1]
    onehots = pair_onehots(routes_ref, experts)
    named = jnp.where(onehots[0] | onehots[1], 1.0, 0.0)
    earlier = lax.broadcasted_iota(jnp.int32, (tok, tok), 0) > lax.broadcasted_iota(
        jnp.int32, (tok, tok), 1
    )
    before = jnp.dot(
        jnp.where(earlier, 1.0, 0.0).astype(BF16), named.astype(BF16), preferred_element_type=F32
    )
    slot_lanes = lax.broadcasted_iota(jnp.int32, (tok, slots), 1)
    picks = []
    for j, ref in enumerate((pick0_ref, pick1_ref)):
        rank = jnp.sum(jnp.where(onehots[j], before, 0.0), axis=1, keepdims=True)
        slot = routes_ref[:, j : j + 1] * (slots // experts) + rank.astype(jnp.int32)
        pick = jnp.where(slot_lanes == slot, 1.0, 0.0)
        ref[...] = pick.astype(BF16)
        picks.append(pick)
    to_slots((picks[0] + picks[1]).astype(BF16), cot_ref[...], out_ref)


def attend_body(head_width, off_ref, qkv_ref, out_ref):
    frames = qkv_ref.shape[0]
    q, k, v = [rows_of(qkv_ref[:, 8 * s : 8 * s + 8, :]).astype(BF16) for s in range(3)]
    rows = frames * 8
    off = off_ref[0]
    same = (
        lax.broadcasted_iota(jnp.int32, (rows, rows), 0) & 7
    ) == (lax.broadcasted_iota(jnp.int32, (rows, rows), 1) & 7)
    lane = lax.broadcasted_iota(jnp.int32, (rows, 256), 1)
    tiles = [jnp.zeros((rows, 128), F32) for _ in range(WIDE // 128)]
    for h in range(H // 2):
        w = h // 2
        first = off + head_width * h - 128 * w
        inside = (lane >= first) & (lane < first + head_width)
        cols = slice(128 * w, 128 * w + 256)
        mine = jnp.where(inside, q[:, cols].astype(F32), 0.0).astype(BF16)
        scores = lax.dot_general(
            mine, k[:, cols], (((1,), (1,)), ((), ())), preferred_element_type=F32
        ) * head_width ** (-0.5)
        scores = jnp.where(same, scores, -1e30)
        peak = jnp.max(scores, axis=1, keepdims=True)
        weights = jnp.exp(scores - peak)
        probs = (weights / jnp.sum(weights, axis=1, keepdims=True)).astype(BF16)
        got = jnp.dot(probs, v[:, cols], preferred_element_type=F32)
        for t in range(2):
            part = slice(128 * t, 128 * t + 128)
            tiles[w + t] = jnp.where(inside[:, part], got[:, part], tiles[w + t])
    for t, tile in enumerate(tiles):
        out_ref[:, :, 128 * t : 128 * t + 128] = blocks_of(tile)


def inv_rms_of(hidden_float):
    return lax.rsqrt(jnp.mean(hidden_float * hidden_float, axis=-1, keepdims=True) + 1e-06)


def project_body(
    att_ref, residual_ref, w_out_ref, gain_ref, w_router_ref, routes_ref, pick0_ref, pick1_ref,
    hidden_ref, combine_ref, out_ref,
):
    low, high = rows_of(att_ref[:, 0]), rows_of(att_ref[:, 1])
    shared = WIDE - STEP
    attended = jnp.concatenate(
        [low[:, :STEP], low[:, STEP:] + high[:, :shared], high[:, shared:]], axis=1
    ).astype(BF16)
    stream = residual_ref[...].astype(F32) + jnp.dot(
        attended, w_out_ref[...], preferred_element_type=F32
    )
    hidden = stream.astype(BF16)
    hidden_ref[...] = hidden
    hidden_float = hidden.astype(F32)
    normed = (hidden_float * inv_rms_of(hidden_float) * gain_ref[...]).astype(BF16)
    to_slots(pick0_ref[...] + pick1_ref[...], normed, out_ref)
    logits = jnp.dot(normed, w_router_ref[...], preferred_element_type=F32)
    onehots = pair_onehots(routes_ref, w_router_ref.shape[1])
    for j in range(2):
        chosen = jnp.sum(jnp.where(onehots[j], logits, 0.0), axis=1, keepdims=True)
        combine_ref[:, j : j + 1] = jax.nn.sigmoid(chosen)


def forward_body(
    expert_ref, x_ref, cot_ref, w_router_ref, gate_ref, up_ref, down_ref,
    out_ref, scaled_ref, units_ref, slope_ref, act_ref,
):
    x = x_ref[...]
    pre_gate = jnp.dot(x, gate_ref[...], preferred_element_type=F32)
    pre_up = jnp.dot(x, up_ref[...], preferred_element_type=F32)
    gate_sig = jax.nn.sigmoid(pre_gate)
    gate_act = pre_gate * gate_sig
    units = (gate_act * pre_up).astype(BF16)
    out_ref[...] = jnp.dot(units, down_ref[...], preferred_element_type=F32).astype(BF16)
    units_ref[...] = units
    slope_ref[...] = pre_up * (gate_sig + gate_act * (1.0 - gate_sig))
    act_ref[...] = gate_act
    logits = jnp.dot(x, w_router_ref[...], preferred_element_type=F32)
    lanes = lax.broadcasted_iota(jnp.int32, logits.shape, 1)
    chosen = jnp.sum(jnp.where(lanes == expert_ref[0], logits, 0.0), axis=1, keepdims=True)
    scaled_ref[...] = (jax.nn.sigmoid(chosen) * cot_ref[...].astype(F32)).astype(BF16)


def backward_body(
    scaled_ref, slope_ref, act_ref, gate_ref, up_ref, down_ref, d_in_ref, d_gate_ref, d_up_ref
):
    turned = (((1,), (1,)), ((), ()))
    d_units = lax.dot_general(
        scaled_ref[...], down_ref[...], turned, preferred_element_type=F32
    )
    d_pre_gate = (d_units * slope_ref[...]).astype(BF16)
    d_pre_up = (d_units * act_ref[...]).astype(BF16)
    d_gate_ref[...] = d_pre_gate
    d_up_ref[...] = d_pre_up
    d_in_ref[...] = (
        lax.dot_general(d_pre_gate, gate_ref[...], turned, preferred_element_type=F32)
        + lax.dot_general(d_pre_up, up_ref[...], turned, preferred_element_type=F32)
    ).astype(BF16)


def pair_sum(ref):
    return (rows_of(ref[:, 0]) + rows_of(ref[:, 1])).astype(BF16)


def output_body(
    back_ref, pick0_ref, pick1_ref, combine_ref, cot_ref, hidden_ref, w_router_ref, routes_ref,
    block_ref, router_ref,
):
    summed = pair_sum(back_ref)
    cotangent = cot_ref[...].astype(F32)
    block = hidden_ref[...].astype(F32)
    onehots = pair_onehots(routes_ref, w_router_ref.shape[1])
    rows = jnp.zeros(onehots[0].shape, F32)
    for j, pick_ref in enumerate((pick0_ref, pick1_ref)):
        combine = combine_ref[:, j : j + 1]
        expert_out = jnp.dot(pick_ref[...], summed, preferred_element_type=F32)
        block = block + combine * expert_out
        d_combine = jnp.sum(cotangent * expert_out, axis=1, keepdims=True)
        rows = rows + jnp.where(onehots[j], d_combine * combine * (1.0 - combine), 0.0)
    block_ref[...] = block.astype(BF16)
    router_ref[...] = lax.dot_general(
        rows,
        w_router_ref[...].astype(F32),
        (((1,), (1,)), ((), ())),
        precision=lax.Precision.HIGHEST,
        preferred_element_type=F32,
    )


def input_body(back_ref, pick0_ref, pick1_ref, router_ref, hidden_ref, gain_ref, cot_ref, out_ref):
    picks = pick0_ref[...] + pick1_ref[...]
    d_normed = router_ref[...] + jnp.dot(picks, pair_sum(back_ref), preferred_element_type=F32)
    hidden_float = hidden_ref[...].astype(F32)
    inv_rms = inv_rms_of(hidden_float)
    gained = d_normed * gain_ref[...]
    d_norm_in = inv_rms * gained - hidden_float * inv_rms**3 * jnp.mean(
        gained * hidden_float, axis=-1, keepdims=True
    )
    out_ref[...] = (cot_ref[...].astype(F32) + d_norm_in).astype(BF16)


def relay(parcel, axes):
    return lax.all_to_all(parcel, axes, split_axis=0, concat_axis=0, tiled=True)


def on_device(
    residual, queries, keys_in, values, w_out, norm_gain, w_router, routes, w_gate, w_up, w_down,
    d_out,
):
    everyone = ("frames", "expert")
    frames = lax.axis_size("frames")
    devices = frames * lax.axis_size("expert")
    width = residual.shape[2]
    tok = residual.shape[0] * residual.shape[1]
    experts = w_router.shape[1]
    cap = 4 * tok // experts
    slots = experts * cap
    hidden_units = w_gate.shape[2]
    smem = pl.BlockSpec(memory_space=pltpu.SMEM)
    vmem = pl.BlockSpec(memory_space=pltpu.VMEM)
    flat = lambda a: a.reshape(tok, width)
    cot = flat(d_out)
    picked = routes.reshape(tok, 2)
    gain = norm_gain.reshape(1, width)
    me = lax.axis_index("frames")
    offset = (me % 2 * (width // 2 - STEP)).reshape(1)
    expert = ((me * lax.axis_size("expert") + lax.axis_index("expert")) // 2).reshape(1)

    packed = call(pack_body, shape((frames, 24, WIDE), BF16), (0, 2 * frames * 24 * WIDE * 2))(
        flat(queries), flat(keys_in), flat(values)
    )
    qkv = relay(packed, "frames")
    parcel = shape((experts, 2, cap, width), BF16)
    pick0, pick1, cot_out = call(
        lambda *refs: route_body(experts, *refs),
        (shape((tok, slots), BF16), shape((tok, slots), BF16), parcel),
        (2 * tok * slots * width, 3 * slots * width * 2),
    )(picked, cot)
    cot_in = relay(cot_out.reshape(devices, cap, width), everyone)
    attended = call(
        lambda *refs: attend_body(width // H, *refs),
        shape((frames, 8, WIDE), BF16),
        (1 << 29, 4 * frames * 8 * WIDE * 2),
        in_specs=[smem, vmem],
    )(offset, qkv)
    attended = relay(attended, "frames").reshape(frames // 2, 2, 8, WIDE)
    hidden, combine, outbound = call(
        project_body,
        (shape((tok, width), BF16), shape((tok, 2), F32), parcel),
        (2 * tok * width * (width + slots), (width + 3 * slots) * width * 2),
    )(attended, flat(residual), w_out, gain, w_router, picked, pick0, pick1)
    arrived = relay(outbound.reshape(devices, cap, width), everyone)

    total = devices * cap
    block = 256
    by_rows = lambda w: pl.BlockSpec((block, w), lambda i: (i, 0))
    whole = lambda a: pl.BlockSpec(a.shape, lambda i: (0, 0))
    gate_w, up_w, down_w = w_gate[0], w_up[0], w_down[0]
    x = arrived.reshape(total, width)
    product = 2 * total * width * hidden_units
    part_out, scaled, units, slope, act = call(
        forward_body,
        (
            shape((total, width), BF16),
            shape((total, width), BF16),
            shape((total, hidden_units), BF16),
            shape((total, hidden_units), F32),
            shape((total, hidden_units), F32),
        ),
        (3 * product, 8 * total * width * 2),
        grid=(total // block,),
        in_specs=[smem, by_rows(width), by_rows(width), whole(w_router), whole(gate_w),
                  whole(up_w), whole(down_w)],
        out_specs=[by_rows(width), by_rows(width)] + [by_rows(hidden_units)] * 3,
    )(expert, x, cot_in.reshape(total, width), w_router, gate_w, up_w, down_w)
    out_back = relay(part_out.reshape(devices, cap, width), everyone)
    part_in, d_pre_gate, d_pre_up = call(
        backward_body,
        (
            shape((total, width), BF16),
            shape((total, hidden_units), BF16),
            shape((total, hidden_units), BF16),
        ),
        (3 * product, 8 * total * width * 2),
        grid=(total // block,),
        in_specs=[by_rows(width), by_rows(hidden_units), by_rows(hidden_units), whole(gate_w),
                  whole(up_w), whole(down_w)],
        out_specs=[by_rows(width), by_rows(hidden_units), by_rows(hidden_units)],
    )(scaled, slope, act, gate_w, up_w, down_w)
    in_back = relay(part_in.reshape(devices, cap, width), everyone)
    d_down = jnp.dot(units.T, scaled, preferred_element_type=F32)
    d_gate = jnp.dot(x.T, d_pre_gate, preferred_element_type=F32)
    d_up = jnp.dot(x.T, d_pre_up, preferred_element_type=F32)

    pairs = (experts, 2, cap, width)
    block_out, router_part = call(
        output_body,
        (shape((tok, width), BF16), shape((tok, width), F32)),
        (4 * tok * width * slots, 4 * slots * width * 2),
    )(out_back.reshape(pairs), pick0, pick1, combine, cot, hidden, w_router, picked)
    d_hidden = call(
        input_body,
        shape((tok, width), BF16),
        (2 * tok * width * slots, 4 * slots * width * 2),
    )(in_back.reshape(pairs), pick0, pick1, router_part, hidden, gain, cot)
    return (
        block_out.reshape(residual.shape),
        d_hidden.reshape(residual.shape),
        d_gate[None],
        d_up[None],
        d_down[None],
    )


def solution(mesh):
    tokens = P("frames", "expert", None)
    weights = P(("frames", "expert"), None, None)
    return jax.shard_map(
        on_device,
        mesh=mesh,
        in_specs=(tokens,) * 4
        + (P(), P(), P(), P("expert", "frames", None, None))
        + (weights,) * 3
        + (tokens,),
        out_specs=(tokens, tokens, weights, weights, weights),
        check_vma=False,
    )
```

profile of v0, /device:TPU:1, one launch (start us, length us, event | category | flops | bytes accessed | tf_op | source)
XLA Modules:
  0.0 214.3 jit_solution(5270504489858348405)
XLA Ops:
  0.6 0.0 copy-start.7
  0.6 1.0 copy-done.7
  1.6 1.0 copy-done.8
  2.6 0.0 copy-start.9
  2.6 1.0 copy-done.9
  3.5 1.0 shard_map.155
  4.5 0.0 copy-start.24
  4.5 0.0 copy-start
  4.5 8.7 %all-to-all-start = ((bf16[32,24,640]{2,1,0:T(8,128)(2,1)}), bf16[32,24,640]{2,1,0:T(8,128)(2,1)S(1)}, u32[]{:S(2)}, u32[]{:S(2)}) async-start(bf16[32,24,640]{2,1,0:T(8,128)(2,1)} %shard_map.155), calls=%async_computation | async-start | bytes 1966080 | tf_op jit(solution)/shard_map/all_to_all | solution.py:228
  13.3 16.5 %all-to-all-done.refs_1_ = bf16[32,24,640]{2,1,0:T(8,128)(2,1)S(1)} async-done(((bf16[32,24,640]{2,1,0:T(8,128)(2,1)}), bf16[32,24,640]{2,1,0:T(8,128)(2,1)S(1)}, u32[]{:S(2)}, u32[]{:S(2)}) %all-to-all-start) | async-done | bytes 983072 | tf_op jit(solution)/shard_map/all_to_all | solution.py:228
  29.7 2.4 %shard_map.156 = bf16[32,8,640]{2,1,0:T(8,128)(2,1)} custom-call(s32[1]{0:T(128)} %bitcast.1.refs_0_, bf16[32,24,640]{2,1,0:T(8,128)(2,1)S(1)} %all-to-all-done.refs_1_), custom_call_target="tpu_custom_call" | custom-call | flops 536870912 | bytes 1310720 | tf_op jit(solution)/shard_map/pallas_call | solution.py:265
  32.1 3.9 %all-to-all-start.1 = ((bf16[32,8,640]{2,1,0:T(8,128)(2,1)}), bf16[32,8,640]{2,1,0:T(8,128)(2,1)S(1)}, u32[]{:S(2)}, u32[]{:S(2)}) async-start(bf16[32,8,640]{2,1,0:T(8,128)(2,1)} %shard_map.156), calls=%async_computation.1 | async-start | bytes 655360 | tf_op jit(solution)/shard_map/all_to_all | solution.py:228
  36.0 0.0 copy-done.24
  36.0 0.1 copy.17
  36.1 0.0 copy-start.2
  36.1 0.0 copy-done
  36.2 2.3 %shard_map.157 = (bf16[128,512]{1,0:T(8,128)(2,1)S(1)}, bf16[128,512]{1,0:T(8,128)(2,1)S(1)}, bf16[64,2,8,1152]{3,2,1,0:T(8,128)(2,1)}) custom-call(s32[128,2]{1,0:T(8,128)S(1)} %bitcast.41, bf16[128,1152]{1,0:T(8,128)(2,1)S(1)} %bitcast.38), custom_call_target="tpu_custom_call" | custom-call | flops 150994944 | bytes 3538944 | tf_op jit(solution)/shard_map/pallas_call | solution.py:259
  38.5 7.2 %all-to-all-done.1 = bf16[32,8,640]{2,1,0:T(8,128)(2,1)S(1)} async-done(((bf16[32,8,640]{2,1,0:T(8,128)(2,1)}), bf16[32,8,640]{2,1,0:T(8,128)(2,1)S(1)}, u32[]{:S(2)}, u32[]{:S(2)}) %all-to-all-start.1) | async-done | bytes 327712 | tf_op jit(solution)/shard_map/all_to_all | solution.py:228
  45.7 0.0 copy-start.23
  45.7 0.0 copy-start.22
  45.7 0.0 copy-start.6
  45.7 7.1 %all-to-all-start.3 = ((bf16[128,8,1152]{2,1,0:T(8,128)(2,1)}), bf16[128,8,1152]{2,1,0:T(8,128)(2,1)}, u32[]{:S(2)}, u32[]{:S(2)}) async-start(bf16[128,8,1152]{2,1,0:T(8,128)(2,1)} %bitcast.11), calls=%async_computation.3 | async-start | bytes 4718592 | tf_op jit(solution)/shard_map/all_to_all | solution.py:228
  52.7 0.0 copy-done.23
  52.8 0.0 copy-done.22
  52.8 0.2 copy.18.w_router_ref
  53.0 0.0 copy-done.2
  53.0 0.0 copy-done.6
  53.0 4.4 %shard_map.158 = (bf16[128,1152]{1,0:T(8,128)(2,1)S(1)}, f32[128,2]{1,0:T(8,128)S(1)}, bf16[64,2,8,1152]{3,2,1,0:T(8,128)(2,1)}) custom-call(bf16[16,2,8,640]{3,2,1,0:T(8,128)(2,1)S(1)} %bitcast.37, bf16[128,1152]{1,0:T(8,128)(2,1)S(1)} %bitcast.44, bf16[1152,1152]{1,0:T(8,128)(2,1)} %w_out_ref.1, f32[1,1152]{1,0:T(1,128)S(1)} %reshape.77.gain_ref, ...), custom_call_target="tpu_custom_call" | custom-call | flops 490733568 | bytes 6193152 | tf_op jit(solution)/shard_map/pallas_call | solution.py:272
  57.4 0.0 copy-start.10
  57.4 0.6 copy-done.10
  58.0 27.8 %all-to-all-done.3 = bf16[128,8,1152]{2,1,0:T(8,128)(2,1)} async-done(((bf16[128,8,1152]{2,1,0:T(8,128)(2,1)}), bf16[128,8,1152]{2,1,0:T(8,128)(2,1)}, u32[]{:S(2)}, u32[]{:S(2)}) %all-to-all-start.3) | async-done | bytes 2359328 | tf_op jit(solution)/shard_map/all_to_all | solution.py:228
  85.8 0.0 copy-start.12
  85.8 0.0 copy-start.14
  85.8 4.9 %all-to-all-start.2 = ((bf16[128,8,1152]{2,1,0:T(8,128)(2,1)}), bf16[128,8,1152]{2,1,0:T(8,128)(2,1)}, u32[]{:S(2)}, u32[]{:S(2)}) async-start(bf16[128,8,1152]{2,1,0:T(8,128)(2,1)} %bitcast.9), calls=%async_computation.2 | async-start | bytes 4718592 | tf_op jit(solution)/shard_map/all_to_all | solution.py:228
  90.7 33.2 %all-to-all-done.2 = bf16[128,8,1152]{2,1,0:T(8,128)(2,1)} async-done(((bf16[128,8,1152]{2,1,0:T(8,128)(2,1)}), bf16[128,8,1152]{2,1,0:T(8,128)(2,1)}, u32[]{:S(2)}, u32[]{:S(2)}) %all-to-all-start.2) | async-done | bytes 2359328 | tf_op jit(solution)/shard_map/all_to_all | solution.py:228
  123.9 0.0 copy-done.12
  123.9 0.0 copy-done.14
  123.9 0.0 copy-start.16
  123.9 1.3 copy-done.16
  125.2 8.7 %shard_map.159 = (bf16[1024,1152]{1,0:T(8,128)(2,1)}, bf16[1024,1152]{1,0:T(8,128)(2,1)}, bf16[1024,512]{1,0:T(8,128)(2,1)S(1)}, f32[1024,512]{1,0:T(8,128)}, f32[1024,512]{1,0:T(8,128)}) custom-call(s32[1]{0:T(128)} %bitcast.expert_ref, bf16[1024,1152]{1,0:T(8,128)(2,1)} %bitcast.10.x_ref, bf16[1024,1152]{1,0:T(8,128)(2,1)} %bitcast.12.cot_ref, ...), custom_call_target="tpu_custom_call" | custom-call | flops 3623878656 | bytes 18874368 | tf_op jit(solution)/shard_map/pallas_call | solution.py:286
  133.9 1.1 copy-done.1
  135.0 3.7 %all-to-all-start.4 = ((bf16[128,8,1152]{2,1,0:T(8,128)(2,1)}), bf16[128,8,1152]{2,1,0:T(8,128)(2,1)S(1)}, u32[]{:S(2)}, u32[]{:S(2)}) async-start(bf16[128,8,1152]{2,1,0:T(8,128)(2,1)} %bitcast.55), calls=%async_computation.4 | async-start | bytes 4718592 | tf_op jit(solution)/shard_map/all_to_all | solution.py:228
  138.7 0.0 copy-start.13
  138.7 1.3 copy-done.13
  140.0 1.3 copy-done.15
  141.3 1.3 copy-done.17
  142.5 8.3 %shard_map.161 = (bf16[1024,1152]{1,0:T(8,128)(2,1)}, bf16[1024,512]{1,0:T(8,128)(2,1)S(1)}, bf16[1024,512]{1,0:T(8,128)(2,1)S(1)}) custom-call(bf16[1024,1152]{1,0:T(8,128)(2,1)} %get-tuple-element.29.scaled_ref, f32[1024,512]{1,0:T(8,128)} %get-tuple-element.30.slope_ref, f32[1024,512]{1,0:T(8,128)} %get-tuple-element.31.act_ref, ...), custom_call_target="tpu_custom_call" | custom-call | flops 3623878656 | bytes 18874368 | tf_op jit(solution)/shard_map/pallas_call | solution.py:302
  150.8 1.1 copy-done.18
  151.9 1.0 copy-done.20
  152.9 19.3 %all-to-all-done.4 = bf16[128,8,1152]{2,1,0:T(8,128)(2,1)S(1)} async-done(((bf16[128,8,1152]{2,1,0:T(8,128)(2,1)}), bf16[128,8,1152]{2,1,0:T(8,128)(2,1)S(1)}, u32[]{:S(2)}, u32[]{:S(2)}) %all-to-all-start.4) | async-done | bytes 2359328 | tf_op jit(solution)/shard_map/all_to_all | solution.py:228
  172.2 4.8 %all-to-all-start.5 = ((bf16[128,8,1152]{2,1,0:T(8,128)(2,1)}), bf16[128,8,1152]{2,1,0:T(8,128)(2,1)}, u32[]{:S(2)}, u32[]{:S(2)}) async-start(bf16[128,8,1152]{2,1,0:T(8,128)(2,1)} %bitcast.54), calls=%async_computation.5 | async-start | bytes 4718592 | tf_op jit(solution)/shard_map/all_to_all | solution.py:228
  177.0 0.0 copy-start.21
  177.1 5.0 %convolution_bitcast_fusion = f32[1,512,1152]{2,1,0:T(8,128)} fusion(bf16[1024,512]{1,0:T(8,128)(2,1)} %copy-done.1, bf16[1024,1152]{1,0:T(8,128)(2,1)} %get-tuple-element.29.scaled_ref), kind=kOutput, calls=%fused_computation | convolution fusion | flops 1207959552 | bytes 5767168 | tf_op jit(solution)/shard_map/dot_general | solution.py:316
  182.1 0.0 copy-done.21
  182.1 4.6 %convolution_bitcast_fusion.2 = f32[1,1152,512]{2,1,0:T(8,128)} fusion(bf16[1024,512]{1,0:T(8,128)(2,1)S(1)} %copy-done.21, bf16[128,8,1152]{2,1,0:T(8,128)(2,1)} %all-to-all-done.2), kind=kOutput, calls=%fused_computation.2 | convolution fusion | flops 1207959552 | bytes 5767168 | tf_op jit(solution)/shard_map/dot_general | solution.py:317
  186.7 0.0 copy-done.19
  186.7 4.5 %convolution_bitcast_fusion.1 = f32[1,1152,512]{2,1,0:T(8,128)} fusion(bf16[1024,512]{1,0:T(8,128)(2,1)S(1)} %copy-done.19, bf16[128,8,1152]{2,1,0:T(8,128)(2,1)} %all-to-all-done.2), kind=kOutput, calls=%fused_computation.1 | convolution fusion | flops 1207959552 | bytes 5767168 | tf_op jit(solution)/shard_map/dot_general | solution.py:318
  191.2 0.0 copy-done.3
  191.2 0.0 copy-done.11
  191.2 2.2 %shard_map.160 = (bf16[128,1152]{1,0:T(8,128)(2,1)}, f32[128,1152]{1,0:T(8,128)S(1)}) custom-call(bf16[64,2,8,1152]{3,2,1,0:T(8,128)(2,1)S(1)} %bitcast.36, bf16[128,512]{1,0:T(8,128)(2,1)S(1)} %get-tuple-element.21.pick0_ref, bf16[128,512]{1,0:T(8,128)(2,1)S(1)} %get-tuple-element.22.pick1_ref, f32[128,2]{1,0:T(8,128)S(1)} %copy-done.11, ...), custom_call_target="tpu_custom_call" | custom-call | flops 301989888 | bytes 4718592 | tf_op jit(solution)/shard_map/pallas_call | solution.py:321
  193.4 0.8 copy-done.4
  194.2 15.9 %all-to-all-done.5 = bf16[128,8,1152]{2,1,0:T(8,128)(2,1)} async-done(((bf16[128,8,1152]{2,1,0:T(8,128)(2,1)}), bf16[128,8,1152]{2,1,0:T(8,128)(2,1)}, u32[]{:S(2)}, u32[]{:S(2)}) %all-to-all-start.5) | async-done | bytes 2359328 | tf_op jit(solution)/shard_map/all_to_all | solution.py:228
  210.1 1.1 copy-done.5
  211.2 3.1 %shard_map.162 = bf16[128,1152]{1,0:T(8,128)(2,1)} custom-call(bf16[64,2,8,1152]{3,2,1,0:T(8,128)(2,1)} %bitcast.20.back_ref, bf16[128,512]{1,0:T(8,128)(2,1)S(1)} %get-tuple-element.21.pick0_ref, bf16[128,512]{1,0:T(8,128)(2,1)S(1)} %get-tuple-element.22.pick1_ref, f32[128,1152]{1,0:T(8,128)S(1)} %copy-done.5, ...), custom_call_target="tpu_custom_call" | custom-call | flops 150994944 | bytes 4718592 | tf_op jit(solution)/shard_map/pallas_call | solution.py:326
  (12 shorter events, 0.0 us)
Async XLA Ops:
  0.6 1.0 copy-start.7
  1.6 1.0 copy-start.8
  2.6 1.0 copy-start.9
  4.5 31.5 %copy-start.24 = (s32[1,1,128,2]{2,3,1,0:T(2,128)S(1)}, s32[1,1,128,2]{2,3,1,0:T(2,128)}, u32[]{:S(2)}) copy-start(s32[1,1,128,2]{2,3,1,0:T(2,128)} %param.19) | copy-start | bytes 3076
  4.5 31.6 %copy-start = (bf16[1,128,1152]{2,1,0:T(8,128)(2,1)S(1)}, bf16[1,128,1152]{2,1,0:T(8,128)(2,1)}, u32[]{:S(2)}) copy-start(bf16[1,128,1152]{2,1,0:T(8,128)(2,1)} %param.23) | copy-start | bytes 884740
  4.5 25.2 %all-to-all-start = ((bf16[32,24,640]{2,1,0:T(8,128)(2,1)}), bf16[32,24,640]{2,1,0:T(8,128)(2,1)S(1)}, u32[]{:S(2)}, u32[]{:S(2)}) async-start(bf16[32,24,640]{2,1,0:T(8,128)(2,1)} %shard_map.155), calls=%async_computation | async-start | bytes 1966080 | tf_op jit(solution)/shard_map/all_to_all | solution.py:228
  32.1 13.6 %all-to-all-start.1 = ((bf16[32,8,640]{2,1,0:T(8,128)(2,1)}), bf16[32,8,640]{2,1,0:T(8,128)(2,1)S(1)}, u32[]{:S(2)}, u32[]{:S(2)}) async-start(bf16[32,8,640]{2,1,0:T(8,128)(2,1)} %shard_map.156), calls=%async_computation.1 | async-start | bytes 655360 | tf_op jit(solution)/shard_map/all_to_all | solution.py:228
  36.1 16.9 %copy-start.2 = (s32[1,1,128,2]{3,2,1,0:T(8,128)}, s32[1,1,128,2]{3,2,1,0:T(8,128)S(1)}, u32[]{:S(2)}) copy-start(s32[1,1,128,2]{3,2,1,0:T(8,128)S(1)} %copy.17) | copy-start | bytes 3076
  45.7 7.1 %copy-start.23 = (f32[1152]{0:T(1024)S(1)}, f32[1152]{0:T(1024)}, u32[]{:S(2)}) copy-start(f32[1152]{0:T(1024)} %param.17) | copy-start | bytes 13828
  45.7 7.1 %copy-start.22 = (bf16[1152,64]{0,1:T(8,128)(2,1)S(1)}, bf16[1152,64]{0,1:T(8,128)(2,1)}, u32[]{:S(2)}) copy-start(bf16[1152,64]{0,1:T(8,128)(2,1)} %param.18) | copy-start | bytes 442372
  45.7 7.3 %copy-start.6 = (bf16[1,128,1152]{2,1,0:T(8,128)(2,1)S(1)}, bf16[1,128,1152]{2,1,0:T(8,128)(2,1)}, u32[]{:S(2)}) copy-start(bf16[1,128,1152]{2,1,0:T(8,128)(2,1)} %param.12) | copy-start | bytes 884740
  45.7 40.1 %all-to-all-start.3 = ((bf16[128,8,1152]{2,1,0:T(8,128)(2,1)}), bf16[128,8,1152]{2,1,0:T(8,128)(2,1)}, u32[]{:S(2)}, u32[]{:S(2)}) async-start(bf16[128,8,1152]{2,1,0:T(8,128)(2,1)} %bitcast.11), calls=%async_computation.3 | async-start | bytes 4718592 | tf_op jit(solution)/shard_map/all_to_all | solution.py:228
  57.4 0.6 copy-start.10
  85.8 38.1 %copy-start.12 = (bf16[1,1152,512]{2,1,0:T(8,128)(2,1)S(1)}, bf16[1,1152,512]{2,1,0:T(8,128)(2,1)}, u32[]{:S(2)}) copy-start(bf16[1,1152,512]{2,1,0:T(8,128)(2,1)} %param.20) | copy-start | bytes 3538948
  85.8 38.1 %copy-start.14 = (bf16[1,1152,512]{2,1,0:T(8,128)(2,1)S(1)}, bf16[1,1152,512]{2,1,0:T(8,128)(2,1)}, u32[]{:S(2)}) copy-start(bf16[1,1152,512]{2,1,0:T(8,128)(2,1)} %param.21) | copy-start | bytes 3538948
  85.8 38.1 %all-to-all-start.2 = ((bf16[128,8,1152]{2,1,0:T(8,128)(2,1)}), bf16[128,8,1152]{2,1,0:T(8,128)(2,1)}, u32[]{:S(2)}, u32[]{:S(2)}) async-start(bf16[128,8,1152]{2,1,0:T(8,128)(2,1)} %bitcast.9), calls=%async_computation.2 | async-start | bytes 4718592 | tf_op jit(solution)/shard_map/all_to_all | solution.py:228
  123.9 1.3 copy-start.16
  133.9 1.1 copy-start.1
  135.0 37.2 %all-to-all-start.4 = ((bf16[128,8,1152]{2,1,0:T(8,128)(2,1)}), bf16[128,8,1152]{2,1,0:T(8,128)(2,1)S(1)}, u32[]{:S(2)}, u32[]{:S(2)}) async-start(bf16[128,8,1152]{2,1,0:T(8,128)(2,1)} %bitcast.55), calls=%async_computation.4 | async-start | bytes 4718592 | tf_op jit(solution)/shard_map/all_to_all | solution.py:228
  138.7 1.3 copy-start.13
  140.0 1.3 copy-start.15
  141.3 1.3 copy-start.17
  150.8 1.1 copy-start.18
  151.9 1.0 copy-start.20
  172.2 37.9 %all-to-all-start.5 = ((bf16[128,8,1152]{2,1,0:T(8,128)(2,1)}), bf16[128,8,1152]{2,1,0:T(8,128)(2,1)}, u32[]{:S(2)}, u32[]{:S(2)}) async-start(bf16[128,8,1152]{2,1,0:T(8,128)(2,1)} %bitcast.54), calls=%async_computation.5 | async-start | bytes 4718592 | tf_op jit(solution)/shard_map/all_to_all | solution.py:228
  177.0 5.0 %copy-start.21 = (bf16[1024,512]{1,0:T(8,128)(2,1)S(1)}, bf16[1024,512]{1,0:T(8,128)(2,1)}, u32[]{:S(2)}) copy-start(bf16[1024,512]{1,0:T(8,128)(2,1)} %copy-done.20) | copy-start | bytes 3145732
  182.1 4.6 %copy-start.19 = (bf16[1024,512]{1,0:T(8,128)(2,1)S(1)}, bf16[1024,512]{1,0:T(8,128)(2,1)}, u32[]{:S(2)}) copy-start(bf16[1024,512]{1,0:T(8,128)(2,1)} %copy-done.18) | copy-start | bytes 3145732
  186.7 4.5 %copy-start.3 = (s32[1,1,128,2]{3,2,1,0:T(8,128)S(1)}, s32[1,1,128,2]{3,2,1,0:T(8,128)}, u32[]{:S(2)}) copy-start(s32[1,1,128,2]{3,2,1,0:T(8,128)} %copy-done.2) | copy-start | bytes 3076
  186.7 4.5 %copy-start.11 = (f32[128,2]{1,0:T(8,128)S(1)}, f32[128,2]{1,0:T(8,128)}, u32[]{:S(2)}) copy-start(f32[128,2]{1,0:T(8,128)} %copy-done.10) | copy-start | bytes 3076
  193.4 0.8 copy-start.4
  210.1 1.1 copy-start.5
where the time goes:
time: 215 us; the launch traced here: 214 us
  waiting for transfers between devices  120 us (56%)
  starting transfers between devices  33.2 us (15%)
  Pallas kernels  32.4 us (15%)
  matrix products  14.1 us (7%)
  local copies, waits for them, and re-layouts  14 us (7%)
    all_to_all x6, waiting for transfers between devices, relay(): return lax.all_to_all(parcel, axes, split_axis=0, concat_axis=0, tiled=True)  120 us
    all_to_all x6, starting transfers between devices, relay(): return lax.all_to_all(parcel, axes, split_axis=0, concat_axis=0, tiled=True)  33.2 us
    unnamed x52, local copies, waits for them, and re-layouts  14 us
    pallas_call x1, Pallas kernels, on_device(): call(forward_body, (shape((total, width), BF16), shape((total, width), BF...  8.74 us
    pallas_call x1, Pallas kernels, on_device(): call(backward_body, (shape((total, width), BF16), shape((total, hidden_un...  8.3 us
    dot_general x1, matrix products, on_device(): d_down = jnp.dot(units.T, scaled, preferred_element_type=F32)  5.03 us
    dot_general x1, matrix products, on_device(): d_gate = jnp.dot(x.T, d_pre_gate, preferred_element_type=F32)  4.58 us
    dot_general x1, matrix products, on_device(): d_up = jnp.dot(x.T, d_pre_up, preferred_element_type=F32)  4.52 us
  transfers between devices with their start and end apart: 6, of which 6 were waited for; matrix products, arithmetic and copies ran while one was open for 7% of the time, Pallas kernels for 8%

commit v1 on v0

v1 whole, which is shorter than its diff:
```python
import jax
import jax.numpy as jnp
from jax import lax
from jax.experimental import pallas as pl
from jax.experimental.pallas import tpu as pltpu
from jax.sharding import PartitionSpec as P

H = 16
F32 = jnp.float32
BF16 = jnp.bfloat16
WIDE = 640
STEP = 512
LIMIT = 48 * 1024 * 1024


def call(body, outs, cost, **extra):
    flops, moved = cost
    return pl.pallas_call(
        body,
        out_shape=outs,
        compiler_params=pltpu.CompilerParams(vmem_limit_bytes=LIMIT),
        cost_estimate=pl.CostEstimate(flops=flops, bytes_accessed=moved, transcendentals=0),
        **extra,
    )


def shape(dims, dtype):
    return jax.ShapeDtypeStruct(dims, dtype)


def rows_of(blocks):
    n, eight, width = blocks.shape
    return blocks.astype(F32).reshape(n * eight, width)


def blocks_of(rows):
    total, width = rows.shape
    return rows.reshape(total // 8, 8, width).astype(BF16)


def pair_onehots(routes_ref, experts):
    tok = routes_ref.shape[0]
    lanes = lax.broadcasted_iota(jnp.int32, (tok, experts), 1)
    return [routes_ref[:, j : j + 1] == lanes for j in range(2)]


def slot_rows(picks, rows, step, store):
    for at in range(0, picks.shape[1], step):
        moved = lax.dot_general(
            picks[:, at : at + step], rows, (((0,), (0,)), ((), ())), preferred_element_type=F32
        )
        store(at // 8, blocks_of(moved))


def pack_body(
    experts, mine_ref, routes_ref, cot_ref, q_ref, k_ref, v_ref,
    out_ref, pick0_ref, pick1_ref, held_ref, sems,
):
    copies = []
    for s, ref in enumerate((q_ref, k_ref, v_ref)):
        for half in range(2):
            copies.append(
                pltpu.make_async_copy(
                    ref.at[:, :, STEP * half : STEP * half + WIDE],
                    out_ref.at[:, half, :, WIDE * s : WIDE * s + WIDE],
                    sems.at[2 * s + half],
                )
            )
            copies[-1].start()
    tok, slots = pick0_ref.shape
    width = cot_ref.shape[1]
    onehots = pair_onehots(routes_ref, experts)
    named = jnp.where(onehots[0] | onehots[1], 1.0, 0.0)
    earlier = lax.broadcasted_iota(jnp.int32, (tok, tok), 0) > lax.broadcasted_iota(
        jnp.int32, (tok, tok), 1
    )
    before = jnp.dot(
        jnp.where(earlier, 1.0, 0.0).astype(BF16), named.astype(BF16), preferred_element_type=F32
    )
    slot_lanes = lax.broadcasted_iota(jnp.int32, (tok, slots), 1)
    picks = []
    for j, ref in enumerate((pick0_ref, pick1_ref)):
        rank = jnp.sum(jnp.where(onehots[j], before, 0.0), axis=1, keepdims=True)
        slot = routes_ref[:, j : j + 1] * (slots // experts) + rank.astype(jnp.int32)
        pick = jnp.where(slot_lanes == slot, 1.0, 0.0)
        ref[...] = pick.astype(BF16)
        picks.append(pick)

    def store(expert, blocks):
        chips = blocks.shape[0] // 4
        held_ref[expert // 4 : expert // 4 + chips] = blocks.reshape(chips, 2, 2, 8, width)

    slot_rows((picks[0] + picks[1]).astype(BF16), cot_ref[...], 128, store)
    for other in range(2):
        at = 3 * WIDE + width * other
        which = mine_ref[0] if other == 0 else 1 - mine_ref[0]
        copies.append(
            pltpu.make_async_copy(
                held_ref.at[:, :, which], out_ref.at[:, :, :, at : at + width], sems.at[6 + other]
            )
        )
        copies[-1].start()
    for copy in copies:
        copy.wait()


def attend_body(head_width, off_ref, qkv_ref, out_ref):
    frames = qkv_ref.shape[0]
    q, k, v = [
        rows_of(qkv_ref[:, :, WIDE * s : WIDE * s + WIDE]).astype(BF16) for s in range(3)
    ]
    rows = frames * 8
    off = off_ref[0]
    same = (
        lax.broadcasted_iota(jnp.int32, (rows, rows), 0) & 7
    ) == (lax.broadcasted_iota(jnp.int32, (rows, rows), 1) & 7)
    lane = lax.broadcasted_iota(jnp.int32, (rows, 256), 1)
    tiles = [jnp.zeros((rows, 128), F32) for _ in range(WIDE // 128)]
    for h in range(H // 2):
        w = h // 2
        first = off + head_width * h - 128 * w
        inside = (lane >= first) & (lane < first + head_width)
        cols = slice(128 * w, 128 * w + 256)
        mine = jnp.where(inside, q[:, cols].astype(F32), 0.0).astype(BF16)
        scores = lax.dot_general(
            mine, k[:, cols], (((1,), (1,)), ((), ())), preferred_element_type=F32
        ) * head_width ** (-0.5)
        scores = jnp.where(same, scores, -1e30)
        peak = jnp.max(scores, axis=1, keepdims=True)
        weights = jnp.exp(scores - peak)
        probs = (weights / jnp.sum(weights, axis=1, keepdims=True)).astype(BF16)
        got = jnp.dot(probs, v[:, cols], preferred_element_type=F32)
        for t in range(2):
            part = slice(128 * t, 128 * t + 128)
            tiles[w + t] = jnp.where(inside[:, part], got[:, part], tiles[w + t])
    for t, tile in enumerate(tiles):
        out_ref[:, :, 128 * t : 128 * t + 128] = blocks_of(tile)


def inv_rms_of(hidden_float):
    return lax.rsqrt(jnp.mean(hidden_float * hidden_float, axis=-1, keepdims=True) + 1e-06)


def project_body(
    att_ref, residual_ref, w_out_ref, gain_ref, w_router_ref, routes_ref, pick0_ref, pick1_ref,
    hidden_ref, combine_ref, out_ref,
):
    low, high = rows_of(att_ref[:, 0]), rows_of(att_ref[:, 1])
    shared = WIDE - STEP
    attended = jnp.concatenate(
        [low[:, :STEP], low[:, STEP:] + high[:, :shared], high[:, shared:]], axis=1
    ).astype(BF16)
    stream = residual_ref[...].astype(F32) + jnp.dot(
        attended, w_out_ref[...], preferred_element_type=F32
    )
    hidden = stream.astype(BF16)
    hidden_ref[...] = hidden
    hidden_float = hidden.astype(F32)
    normed = (hidden_float * inv_rms_of(hidden_float) * gain_ref[...]).astype(BF16)

    def store(expert, blocks):
        for half in range(2):
            out_ref[expert : expert + blocks.shape[0], half] = blocks

    slot_rows(pick0_ref[...] + pick1_ref[...], normed, 128, store)
    logits = jnp.dot(normed, w_router_ref[...], preferred_element_type=F32)
    onehots = pair_onehots(routes_ref, w_router_ref.shape[1])
    for j in range(2):
        chosen = jnp.sum(jnp.where(onehots[j], logits, 0.0), axis=1, keepdims=True)
        combine_ref[:, j : j + 1] = jax.nn.sigmoid(chosen)


def expert_body(
    place_ref, x_ref, cot0_ref, cot1_ref, cot2_ref, cot3_ref, w_router_ref, gate_ref, up_ref,
    down_ref, out_ref, scaled_ref, units_ref, d_gate_ref, d_up_ref, cot_ref,
):
    turned = (((1,), (1,)), ((), ()))
    for n, ref in enumerate((cot0_ref, cot1_ref, cot2_ref, cot3_ref)):
        cot_ref[:, place_ref[1 + n]] = ref[...]
    frames, planes, eight, width = cot_ref.shape
    x = x_ref[...]
    pre_gate = jnp.dot(x, gate_ref[...], preferred_element_type=F32)
    pre_up = jnp.dot(x, up_ref[...], preferred_element_type=F32)
    gate_sig = jax.nn.sigmoid(pre_gate)
    gate_act = pre_gate * gate_sig
    units = (gate_act * pre_up).astype(BF16)
    units_ref[...] = units
    out_ref[:, :eight] = blocks_of(jnp.dot(units, down_ref[...], preferred_element_type=F32))
    logits = jnp.dot(x, w_router_ref[...], preferred_element_type=F32)
    lanes = lax.broadcasted_iota(jnp.int32, logits.shape, 1)
    chosen = jnp.sum(jnp.where(lanes == place_ref[0], logits, 0.0), axis=1, keepdims=True)
    cotangent = rows_of(cot_ref[...].reshape(frames * planes, eight, width))
    scaled = (jax.nn.sigmoid(chosen) * cotangent).astype(BF16)
    scaled_ref[...] = scaled
    d_units = lax.dot_general(scaled, down_ref[...], turned, preferred_element_type=F32)
    slope = pre_up * (gate_sig + gate_act * (1.0 - gate_sig))
    d_pre_gate = (d_units * slope).astype(BF16)
    d_pre_up = (d_units * gate_act).astype(BF16)
    d_gate_ref[...] = d_pre_gate
    d_up_ref[...] = d_pre_up
    out_ref[:, eight:] = blocks_of(
        lax.dot_general(d_pre_gate, gate_ref[...], turned, preferred_element_type=F32)
        + lax.dot_general(d_pre_up, up_ref[...], turned, preferred_element_type=F32)
    )


def pair_sum(ref, rows):
    return (rows_of(ref[:, 0, rows]) + rows_of(ref[:, 1, rows])).astype(BF16)


def finish_body(
    back_ref, pick0_ref, pick1_ref, combine_ref, cot_ref, hidden_ref, gain_ref, w_router_ref,
    routes_ref, block_ref, d_hidden_ref, got_ref,
):
    step = pl.program_id(0)
    outs = pair_sum(back_ref, slice(0, 8))
    ins = pair_sum(back_ref, slice(8, 16))
    picks = [pick0_ref[...], pick1_ref[...]]
    new = [
        jnp.dot(picks[0], outs, preferred_element_type=F32),
        jnp.dot(picks[1], outs, preferred_element_type=F32),
        jnp.dot(picks[0] + picks[1], ins, preferred_element_type=F32),
    ]

    @pl.when(step == 0)
    def _():
        for n in range(3):
            got_ref[n] = new[n]

    @pl.when(step > 0)
    def _():
        for n in range(3):
            got_ref[n] = got_ref[n] + new[n]

    @pl.when(step == pl.num_programs(0) - 1)
    def _():
        cotangent = cot_ref[...].astype(F32)
        hidden_float = hidden_ref[...].astype(F32)
        block = hidden_float
        onehots = pair_onehots(routes_ref, w_router_ref.shape[1])
        rows = jnp.zeros(onehots[0].shape, F32)
        for j in range(2):
            combine = combine_ref[:, j : j + 1]
            expert_out = got_ref[j]
            block = block + combine * expert_out
            d_combine = jnp.sum(cotangent * expert_out, axis=1, keepdims=True)
            rows = rows + jnp.where(onehots[j], d_combine * combine * (1.0 - combine), 0.0)
        block_ref[...] = block.astype(BF16)
        d_normed = got_ref[2] + lax.dot_general(
            rows,
            w_router_ref[...].astype(F32),
            (((1,), (1,)), ((), ())),
            precision=lax.Precision.HIGHEST,
            preferred_element_type=F32,
        )
        inv_rms = inv_rms_of(hidden_float)
        gained = d_normed * gain_ref[...]
        d_norm_in = inv_rms * gained - hidden_float * inv_rms**3 * jnp.mean(
            gained * hidden_float, axis=-1, keepdims=True
        )
        d_hidden_ref[...] = (cotangent + d_norm_in).astype(BF16)


def relay(parcel, axes):
    return lax.all_to_all(parcel, axes, split_axis=0, concat_axis=0, tiled=True)


def on_device(
    residual, queries, keys_in, values, w_out, norm_gain, w_router, routes, w_gate, w_up, w_down,
    d_out,
):
    everyone = ("frames", "expert")
    frames = lax.axis_size("frames")
    devices = frames * lax.axis_size("expert")
    width = residual.shape[2]
    tok = residual.shape[0] * residual.shape[1]
    experts = w_router.shape[1]
    cap = 4 * tok // experts
    slots = experts * cap
    hidden_units = w_gate.shape[2]
    smem = pl.BlockSpec(memory_space=pltpu.SMEM)
    vmem = pl.BlockSpec(memory_space=pltpu.VMEM)
    anywhere = pl.BlockSpec(memory_space=pl.ANY)
    flat = lambda a: a.reshape(tok, width)
    eights = lambda a: a.reshape(tok // 8, 8, width)
    cot = flat(d_out)
    picked = routes.reshape(tok, 2)
    gain = norm_gain.reshape(1, width)
    me, plane = lax.axis_index("frames"), lax.axis_index("expert")
    offset = (me % 2 * (width // 2 - STEP)).reshape(1)

    full = 3 * WIDE + 2 * width
    packed, pick0, pick1 = call(
        lambda *refs: pack_body(experts, *refs),
        (shape((frames // 2, 2, 8, full), BF16), shape((tok, slots), BF16),
         shape((tok, slots), BF16)),
        (2 * tok * slots * width, 2 * frames * 8 * full * 2),
        in_specs=[smem, vmem, vmem, anywhere, anywhere, anywhere],
        out_specs=(anywhere, vmem, vmem),
        scratch_shapes=[
            pltpu.VMEM((frames // 2, 2, 2, 8, width), BF16),
            pltpu.SemaphoreType.DMA((8,)),
        ],
    )((plane // 2).reshape(1), picked, cot, eights(queries), eights(keys_in), eights(values))
    mixed = relay(packed.reshape(frames, 8, full), "frames")
    attended = call(
        lambda *refs: attend_body(width // H, *refs),
        shape((frames, 8, WIDE), BF16),
        (1 << 29, 4 * frames * 8 * WIDE * 2),
        grid=(1,),
        in_specs=[smem, pl.BlockSpec((frames, 8, 3 * WIDE), lambda i: (0, 0, 0))],
        out_specs=pl.BlockSpec((frames, 8, WIDE), lambda i: (0, 0, 0)),
    )(offset, mixed)
    attended = relay(attended, "frames").reshape(frames // 2, 2, 8, WIDE)
    near = [(0, 1), (1, 0), (2, 3), (3, 2)]
    far = [(0, 3), (3, 0), (1, 2), (2, 1)]
    cots = [mixed[:, :, 3 * WIDE : 3 * WIDE + width]]
    cots.append(lax.ppermute(cots[0], "expert", near))
    cots.append(lax.ppermute(mixed[:, :, 3 * WIDE + width :], "expert", far))
    cots.append(lax.ppermute(cots[2], "expert", near))
    hidden, combine, outbound = call(
        project_body,
        (shape((tok, width), BF16), shape((tok, 2), F32), shape((experts, 2, cap, width), BF16)),
        (2 * tok * width * (width + slots), (width + 3 * slots) * width * 2),
    )(attended, flat(residual), w_out, gain, w_router, picked, pick0, pick1)
    arrived = relay(outbound.reshape(devices, cap, width), everyone)

    total = devices * cap
    block = 256
    by_rows = lambda w: pl.BlockSpec((block, w), lambda i: (i, 0))
    by_blocks = lambda n, m: pl.BlockSpec((n, m, width), lambda i: (i, 0, 0))
    whole = lambda a: pl.BlockSpec(a.shape, lambda i: (0, 0))
    gate_w, up_w, down_w = w_gate[0], w_up[0], w_down[0]
    x = arrived.reshape(total, width)
    product = 2 * total * width * hidden_units
    place = jnp.stack(
        [(me * 4 + plane) // 2, plane, plane ^ 1, 3 - plane, (3 - plane) ^ 1]
    ).astype(jnp.int32)
    per = block // 32
    returned, scaled, units, d_pre_gate, d_pre_up = call(
        expert_body,
        (
            shape((devices, 2 * cap, width), BF16),
            shape((total, width), BF16),
            shape((total, hidden_units), BF16),
            shape((total, hidden_units), BF16),
            shape((total, hidden_units), BF16),
        ),
        (6 * product, 10 * total * width * 2),
        grid=(total // block,),
        in_specs=[smem, by_rows(width)] + [by_blocks(per, 8)] * 4
        + [whole(w_router), whole(gate_w), whole(up_w), whole(down_w)],
        out_specs=[by_blocks(block // 8, 2 * cap), by_rows(width)] + [by_rows(hidden_units)] * 3,
        scratch_shapes=[pltpu.VMEM((per, 4, 8, width), BF16)],
    )(place, x, *cots, w_router, gate_w, up_w, down_w)
    back = relay(returned, everyone).reshape(experts, 2, 2 * cap, width)
    d_down = jnp.dot(units.T, scaled, preferred_element_type=F32)
    d_gate = jnp.dot(x.T, d_pre_gate, preferred_element_type=F32)
    d_up = jnp.dot(x.T, d_pre_up, preferred_element_type=F32)

    part = experts // 4
    by_slots = pl.BlockSpec((tok, part * cap), lambda i: (0, i))
    block_out, d_hidden = call(
        finish_body,
        (shape((tok, width), BF16), shape((tok, width), BF16)),
        (6 * tok * width * slots, 4 * slots * width * 2),
        grid=(4,),
        in_specs=[
            pl.BlockSpec((part, 2, 2 * cap, width), lambda i: (i, 0, 0, 0)), by_slots, by_slots,
            whole(combine), whole(cot), whole(hidden), whole(gain), whole(w_router),
            whole(picked),
        ],
        out_specs=(whole(cot), whole(cot)),
        scratch_shapes=[pltpu.VMEM((3, tok, width), F32)],
    )(back, pick0, pick1, combine, cot, hidden, gain, w_router, picked)
    return (
        block_out.reshape(residual.shape),
        d_hidden.reshape(residual.shape),
        d_gate[None],
        d_up[None],
        d_down[None],
    )


def solution(mesh):
    tokens = P("frames", "expert", None)
    weights = P(("frames", "expert"), None, None)
    return jax.shard_map(
        on_device,
        mesh=mesh,
        in_specs=(tokens,) * 4
        + (P(), P(), P(), P("expert", "frames", None, None))
        + (weights,) * 3
        + (tokens,),
        out_specs=(tokens, tokens, weights, weights, weights),
        check_vma=False,
    )
```

time: 215 us -> 224 us (1.042)
  waiting for transfers between devices: 120 us -> 134 us
  Pallas kernels: 32.4 us -> 28.5 us
    ppermute x0 -> x3, waiting for transfers between devices: none -> 51.9 us  [the longest x1 37.9 us: on_device(): cots.append(lax.ppermute(mixed[:, :, 3 * WIDE + width:], 'expert', far))]
    all_to_all x6 -> x4, waiting for transfers between devices: 120 us -> 81.8 us  [relay(): return lax.all_to_all(parcel, axes, split_axis=0, concat_axis=0, tiled=True)]
    pallas_call x7 -> x4, Pallas kernels: 30.1 us -> 26.2 us  [the longest x1 15.7 us: on_device(): call(expert_body, (shape((devices, 2 * cap, width), BF16), shape((total,...]
    ppermute x0 -> x3, starting transfers between devices: none -> 3.34 us  [the longest x1 3.34 us: on_device(): cots.append(lax.ppermute(mixed[:, :, 3 * WIDE + width:], 'expert', far))]
    all_to_all x6 -> x4, starting transfers between devices: 33.2 us -> 30 us  [relay(): return lax.all_to_all(parcel, axes, split_axis=0, concat_axis=0, tiled=True)]
    unnamed x52 -> x44, local copies, waits for them, and re-layouts: 14 us -> 12.2 us
  transfers between devices with their start and end apart: 6 -> 7, of which waited for: 6 -> 5; matrix products, arithmetic and copies ran while one was open for 7% -> 7% of each run, Pallas kernels for 8% -> 0%
where the time goes in v1:
time: 224 us; the launch traced here: 223 us
  waiting for transfers between devices  134 us (60%)
  starting transfers between devices  33.3 us (15%)
  Pallas kernels  28.5 us (13%)
  matrix products  13.9 us (6%)
  local copies, waits for them, and re-layouts  13.1 us (6%)
    all_to_all x4, waiting for transfers between devices, relay(): return lax.all_to_all(parcel, axes, split_axis=0, concat_axis=0, tiled=True)  81.8 us
    ppermute x1, waiting for transfers between devices, on_device(): cots.append(lax.ppermute(mixed[:, :, 3 * WIDE + width:], 'expert', far))  37.9 us
    all_to_all x4, starting transfers between devices, relay(): return lax.all_to_all(parcel, axes, split_axis=0, concat_axis=0, tiled=True)  30 us
    pallas_call x1, Pallas kernels, on_device(): call(expert_body, (shape((devices, 2 * cap, width), BF16), shape((total,...  15.7 us
    ppermute x1, waiting for transfers between devices, on_device(): cots.append(lax.ppermute(cots[2], 'expert', near))  14 us
    unnamed x44, local copies, waits for them, and re-layouts  12.2 us
    pallas_call x1, Pallas kernels, on_device(): call(finish_body, (shape((tok, width), BF16), shape((tok, width), BF16)),...  6.23 us
    dot_general x1, matrix products, on_device(): d_down = jnp.dot(units.T, scaled, preferred_element_type=F32)  4.72 us
  transfers between devices with their start and end apart: 7, of which 5 were waited for; matrix products, arithmetic and copies ran while one was open for 7% of the time, Pallas kernels for 0%

profile of v1, /device:TPU:1, one launch (start us, length us, event | category | flops | bytes accessed | tf_op | source)
XLA Modules:
  0.0 223.4 jit_solution(4841218769109088296)
XLA Ops:
  0.6 0.8 copy.17
  1.4 0.0 copy-start.2
  1.4 1.0 copy-done.2
  2.4 0.0 copy-start.9
  2.4 1.0 copy-done.9
  3.4 0.0 copy-start.10
  3.4 1.0 copy-done.10
  4.3 0.0 copy-start.11
  4.3 1.0 copy-done.11
  5.3 1.2 shard_map.155
  6.5 0.0 copy-start.1
  6.5 1.3 copy-done.1
  7.8 0.0 copy-start.4
  7.8 0.0 copy-start.6
  7.8 8.6 %all-to-all-start = ((bf16[32,8,4224]{2,1,0:T(8,128)(2,1)}), bf16[32,8,4224]{2,1,0:T(8,128)(2,1)S(1)}, u32[]{:S(2)}, u32[]{:S(2)}) async-start(bf16[32,8,4224]{2,1,0:T(8,128)(2,1)} %bitcast.38), calls=%async_computation | async-start | bytes 4325376 | tf_op jit(solution)/shard_map/all_to_all | solution.py:265
  16.4 0.0 copy-start.20
  16.4 0.0 copy-start.8
  16.5 28.5 %all-to-all-done.refs_1_ = bf16[32,8,4224]{2,1,0:T(8,128)(2,1)S(1)} async-done(((bf16[32,8,4224]{2,1,0:T(8,128)(2,1)}), bf16[32,8,4224]{2,1,0:T(8,128)(2,1)S(1)}, u32[]{:S(2)}, u32[]{:S(2)}) %all-to-all-start) | async-done | bytes 2162720 | tf_op jit(solution)/shard_map/all_to_all | solution.py:265
  45.0 2.3 %shard_map.156 = bf16[32,8,640]{2,1,0:T(8,128)(2,1)} custom-call(s32[1]{0:T(128)} %bitcast.5.refs_0_, bf16[32,8,4224]{2,1,0:T(8,128)(2,1)S(1)} %all-to-all-done.refs_1_), custom_call_target="tpu_custom_call" | custom-call | flops 536870912 | bytes 1310720 | tf_op jit(solution)/shard_map/pallas_call | solution.py:306
  47.3 5.9 %all-to-all-start.1 = ((bf16[32,8,640]{2,1,0:T(8,128)(2,1)}), bf16[32,8,640]{2,1,0:T(8,128)(2,1)S(1)}, u32[]{:S(2)}, u32[]{:S(2)}) async-start(bf16[32,8,640]{2,1,0:T(8,128)(2,1)} %shard_map.156), calls=%async_computation.1 | async-start | bytes 655360 | tf_op jit(solution)/shard_map/all_to_all | solution.py:265
  53.2 0.0 copy-done.20
  53.2 0.2 copy.18.w_router_ref
  53.5 0.7 reshape.68.gain_ref
  54.2 8.7 %all-to-all-done.1 = bf16[32,8,640]{2,1,0:T(8,128)(2,1)S(1)} async-done(((bf16[32,8,640]{2,1,0:T(8,128)(2,1)}), bf16[32,8,640]{2,1,0:T(8,128)(2,1)S(1)}, u32[]{:S(2)}, u32[]{:S(2)}) %all-to-all-start.1) | async-done | bytes 327712 | tf_op jit(solution)/shard_map/all_to_all | solution.py:265
  62.9 0.0 copy-done.4
  62.9 0.0 copy-done.6
  62.9 0.0 copy-done.8
  62.9 3.1 %shard_map.157 = (bf16[128,1152]{1,0:T(8,128)(2,1)S(1)}, f32[128,2]{1,0:T(8,128)S(1)}, bf16[64,2,8,1152]{3,2,1,0:T(8,128)(2,1)S(1)}) custom-call(bf16[16,2,8,640]{3,2,1,0:T(8,128)(2,1)S(1)} %bitcast.39, bf16[128,1152]{1,0:T(8,128)(2,1)S(1)} %bitcast.45, bf16[1152,1152]{1,0:T(8,128)(2,1)} %w_out_ref.1, f32[1,1152]{1,0:T(1,128)S(1)} %reshape.68.gain_ref, ...), custom_call_target="tpu_custom_call" | custom-call | flops 490733568 | bytes 6193152 | tf_op jit(solution)/shard_map/pallas_call | solution.py:321
  66.0 0.0 copy-start
  66.0 1.4 copy-done
  67.4 0.0 copy-start.12
  67.4 0.7 copy-done.12
  68.2 7.1 %all-to-all-start.2 = ((bf16[128,8,1152]{2,1,0:T(8,128)(2,1)}), bf16[128,8,1152]{2,1,0:T(8,128)(2,1)}, u32[]{:S(2)}, u32[]{:S(2)}) async-start(bf16[128,8,1152]{2,1,0:T(8,128)(2,1)} %bitcast.37), calls=%async_computation.2 | async-start | bytes 4718592 | tf_op jit(solution)/shard_map/all_to_all | solution.py:265
  75.2 0.1 fusion.2
  75.3 3.3 %collective-permute-start.1 = (bf16[32,8,1152]{2,1,0:T(8,128)(2,1)S(1)}, bf16[32,8,1152]{2,1,0:T(8,128)(2,1)S(1)}, u32[]{:S(2)}, u32[]{:S(2)}) collective-permute-start(bf16[32,8,1152]{2,1,0:T(8,128)(2,1)S(1)} %get-tuple-element.31), channel_id=1, source_target_pairs={{0,3},{3,0},{1,2},{2,1},{4,7},{7,4},{5,6},{6,5},{8,11},{11,8},{9,1... | collective-permute-start | bytes 1769480 | tf_op jit(solution)/shard_map/ppermute | solution.py:319
  78.7 0.0 collective-permute-start
  78.7 37.9 %collective-permute-done.1.cot2_ref = bf16[32,8,1152]{2,1,0:T(8,128)(2,1)S(1)} collective-permute-done((bf16[32,8,1152]{2,1,0:T(8,128)(2,1)S(1)}, bf16[32,8,1152]{2,1,0:T(8,128)(2,1)S(1)}, u32[]{:S(2)}, u32[]{:S(2)}) %collective-permute-start.1) | collective-permute-done | bytes 589856 | tf_op jit(solution)/shard_map/ppermute | solution.py:319
  116.6 0.0 collective-permute-start.2
  116.6 0.1 stack.23.place_ref
  116.6 0.0 collective-permute-done.cot1_ref
  116.6 14.0 %collective-permute-done.2.cot3_ref = bf16[32,8,1152]{2,1,0:T(8,128)(2,1)S(1)} collective-permute-done((bf16[32,8,1152]{2,1,0:T(8,128)(2,1)S(1)}, bf16[32,8,1152]{2,1,0:T(8,128)(2,1)S(1)}, u32[]{:S(2)}, u32[]{:S(2)}) %collective-permute-start.2) | collective-permute-done | bytes 589856 | tf_op jit(solution)/shard_map/ppermute | solution.py:320
  130.6 0.0 copy-start.14
  130.6 0.8 copy-done.14
  131.4 0.0 all-to-all-done.2
  131.4 0.0 copy-start.15
  131.4 1.1 copy-done.15
  132.5 15.7 %shard_map.158 = (bf16[128,16,1152]{2,1,0:T(8,128)(2,1)}, bf16[1024,1152]{1,0:T(8,128)(2,1)}, bf16[1024,512]{1,0:T(8,128)(2,1)S(1)}, bf16[1024,512]{1,0:T(8,128)(2,1)S(1)}, bf16[1024,512]{1,0:T(8,128)(2,1)S(1)}) custom-call(s32[5]{0:T(128)S(1)} %stack.23.place_ref, bf16[1024,1152]{1,0:T(8,128)(2,1)} %bitcast.16.x_ref, ...), custom_call_target="tpu_custom_call" | custom-call | flops 7247757312 | bytes 23592960 | tf_op jit(solution)/shard_map/pallas_call | solution.py:340
  148.2 0.0 copy-start.16
  148.2 1.0 copy-done.16
  149.2 1.0 copy-done.18
  150.2 8.4 %all-to-all-start.3 = ((bf16[128,16,1152]{2,1,0:T(8,128)(2,1)}), bf16[128,16,1152]{2,1,0:T(8,128)(2,1)}, u32[]{:S(2)}, u32[]{:S(2)}) async-start(bf16[128,16,1152]{2,1,0:T(8,128)(2,1)} %get-tuple-element.22), calls=%async_computation.3 | async-start | bytes 9437184 | tf_op jit(solution)/shard_map/all_to_all | solution.py:265
  158.6 0.0 copy-start.19
  158.6 4.7 %convolution_bitcast_fusion = f32[1,512,1152]{2,1,0:T(8,128)} fusion(bf16[1024,512]{1,0:T(8,128)(2,1)S(1)} %get-tuple-element.29, bf16[1024,1152]{1,0:T(8,128)(2,1)} %get-tuple-element.30), kind=kOutput, calls=%fused_computation | convolution fusion | flops 1207959552 | bytes 5767168 | tf_op jit(solution)/shard_map/dot_general | solution.py:357
  163.3 0.0 copy-done.19
  163.3 4.6 %convolution_bitcast_fusion.1 = f32[1,1152,512]{2,1,0:T(8,128)} fusion(bf16[1024,512]{1,0:T(8,128)(2,1)S(1)} %copy-done.19, bf16[128,8,1152]{2,1,0:T(8,128)(2,1)} %all-to-all-done.2), kind=kOutput, calls=%fused_computation.1 | convolution fusion | flops 1207959552 | bytes 5767168 | tf_op jit(solution)/shard_map/dot_general | solution.py:359
  167.9 0.0 copy-done.17
  167.9 0.0 copy-start.13
  167.9 4.6 %convolution_bitcast_fusion.2 = f32[1,1152,512]{2,1,0:T(8,128)} fusion(bf16[1024,512]{1,0:T(8,128)(2,1)S(1)} %copy-done.17, bf16[128,8,1152]{2,1,0:T(8,128)(2,1)} %all-to-all-done.2), kind=kOutput, calls=%fused_computation.2 | convolution fusion | flops 1207959552 | bytes 5767168 | tf_op jit(solution)/shard_map/dot_general | solution.py:358
  172.5 44.6 %all-to-all-done.3 = bf16[128,16,1152]{2,1,0:T(8,128)(2,1)} async-done(((bf16[128,16,1152]{2,1,0:T(8,128)(2,1)}), bf16[128,16,1152]{2,1,0:T(8,128)(2,1)}, u32[]{:S(2)}, u32[]{:S(2)}) %all-to-all-start.3) | async-done | bytes 4718624 | tf_op jit(solution)/shard_map/all_to_all | solution.py:265
  217.1 0.0 copy-done.3
  217.1 0.0 copy-done.5
  217.1 0.0 copy-done.7
  217.1 0.0 copy-done.13
  217.1 6.2 %shard_map.159 = (bf16[128,1152]{1,0:T(8,128)(2,1)}, bf16[128,1152]{1,0:T(8,128)(2,1)}) custom-call(bf16[64,2,16,1152]{3,2,1,0:T(8,128)(2,1)} %bitcast.20.back_ref, bf16[128,512]{1,0:T(8,128)(2,1)S(1)} %copy-done.5, bf16[128,512]{1,0:T(8,128)(2,1)S(1)} %copy-done.7, f32[128,2]{1,0:T(8,128)S(1)} %get-tuple-element.23.combine_ref, ...), custom_call_target="tpu_custom_call" | custom-call | flops 452984832 | bytes 4718592 | tf_op jit(solution)/shard_map/pallas_call | solution.py:363
  (5 shorter events, 0.0 us)
Async XLA Ops:
  1.4 1.0 copy-start.2
  2.4 1.0 copy-start.9
  3.4 1.0 copy-start.10
  4.3 1.0 copy-start.11
  6.5 1.3 copy-start.1
  7.8 55.1 %copy-start.4 = (bf16[128,512]{1,0:T(8,128)(2,1)}, bf16[128,512]{1,0:T(8,128)(2,1)S(1)}, u32[]{:S(2)}) copy-start(bf16[128,512]{1,0:T(8,128)(2,1)S(1)} %get-tuple-element.19.pick0_ref) | copy-start | bytes 393220
  7.8 55.1 %copy-start.6 = (bf16[128,512]{1,0:T(8,128)(2,1)}, bf16[128,512]{1,0:T(8,128)(2,1)S(1)}, u32[]{:S(2)}) copy-start(bf16[128,512]{1,0:T(8,128)(2,1)S(1)} %get-tuple-element.20.pick1_ref) | copy-start | bytes 393220
  7.8 37.2 %all-to-all-start = ((bf16[32,8,4224]{2,1,0:T(8,128)(2,1)}), bf16[32,8,4224]{2,1,0:T(8,128)(2,1)S(1)}, u32[]{:S(2)}, u32[]{:S(2)}) async-start(bf16[32,8,4224]{2,1,0:T(8,128)(2,1)} %bitcast.38), calls=%async_computation | async-start | bytes 4325376 | tf_op jit(solution)/shard_map/all_to_all | solution.py:265
  16.4 36.8 %copy-start.20 = (bf16[1152,64]{0,1:T(8,128)(2,1)S(1)}, bf16[1152,64]{0,1:T(8,128)(2,1)}, u32[]{:S(2)}) copy-start(bf16[1152,64]{0,1:T(8,128)(2,1)} %param.18) | copy-start | bytes 442372
  16.4 46.5 %copy-start.8 = (bf16[1,128,1152]{2,1,0:T(8,128)(2,1)S(1)}, bf16[1,128,1152]{2,1,0:T(8,128)(2,1)}, u32[]{:S(2)}) copy-start(bf16[1,128,1152]{2,1,0:T(8,128)(2,1)} %param.12) | copy-start | bytes 884740
  47.3 15.6 %all-to-all-start.1 = ((bf16[32,8,640]{2,1,0:T(8,128)(2,1)}), bf16[32,8,640]{2,1,0:T(8,128)(2,1)S(1)}, u32[]{:S(2)}, u32[]{:S(2)}) async-start(bf16[32,8,640]{2,1,0:T(8,128)(2,1)} %shard_map.156), calls=%async_computation.1 | async-start | bytes 655360 | tf_op jit(solution)/shard_map/all_to_all | solution.py:265
  66.0 1.4 copy-start
  67.4 0.7 copy-start.12
  68.2 63.3 %all-to-all-start.2 = ((bf16[128,8,1152]{2,1,0:T(8,128)(2,1)}), bf16[128,8,1152]{2,1,0:T(8,128)(2,1)}, u32[]{:S(2)}, u32[]{:S(2)}) async-start(bf16[128,8,1152]{2,1,0:T(8,128)(2,1)} %bitcast.37), calls=%async_computation.2 | async-start | bytes 4718592 | tf_op jit(solution)/shard_map/all_to_all | solution.py:265
  75.3 41.2 %collective-permute-start.1 = (bf16[32,8,1152]{2,1,0:T(8,128)(2,1)S(1)}, bf16[32,8,1152]{2,1,0:T(8,128)(2,1)S(1)}, u32[]{:S(2)}, u32[]{:S(2)}) collective-permute-start(bf16[32,8,1152]{2,1,0:T(8,128)(2,1)S(1)} %get-tuple-element.31), channel_id=1, source_target_pairs={{0,3},{3,0},{1,2},{2,1},{4,7},{7,4},{5,6},{6,5},{8,11},{11,8},{9,1... | collective-permute-start | bytes 1769480 | tf_op jit(solution)/shard_map/ppermute | solution.py:319
  78.7 38.0 %collective-permute-start = (bf16[32,8,1152]{2,1,0:T(8,128)(2,1)S(1)}, bf16[32,8,1152]{2,1,0:T(8,128)(2,1)S(1)}, u32[]{:S(2)}, u32[]{:S(2)}) collective-permute-start(bf16[32,8,1152]{2,1,0:T(8,128)(2,1)S(1)} %get-tuple-element.32.cot0_ref), channel_id=1, source_target_pairs={{0,1},{1,0},{2,3},{3,2},{4,5},{5,4},{6,7},{7,6},{8,9},{9,8},{10,11... | collective-permute-start | bytes 1769480 | tf_op jit(solution)/shard_map/ppermute | solution.py:318
  116.6 14.1 %collective-permute-start.2 = (bf16[32,8,1152]{2,1,0:T(8,128)(2,1)S(1)}, bf16[32,8,1152]{2,1,0:T(8,128)(2,1)S(1)}, u32[]{:S(2)}, u32[]{:S(2)}) collective-permute-start(bf16[32,8,1152]{2,1,0:T(8,128)(2,1)S(1)} %collective-permute-done.1.cot2_ref), channel_id=1, source_target_pairs={{0,1},{1,0},{2,3},{3,2},{4,5},{5,4},{6,7},{7,6},{8,9},{9,8},{10,11... | collective-permute-start | bytes 1769480 | tf_op jit(solution)/shard_map/ppermute | solution.py:320
  130.6 0.8 copy-start.14
  131.4 1.1 copy-start.15
  148.2 1.0 copy-start.16
  149.2 1.0 copy-start.18
  150.2 66.9 %all-to-all-start.3 = ((bf16[128,16,1152]{2,1,0:T(8,128)(2,1)}), bf16[128,16,1152]{2,1,0:T(8,128)(2,1)}, u32[]{:S(2)}, u32[]{:S(2)}) async-start(bf16[128,16,1152]{2,1,0:T(8,128)(2,1)} %get-tuple-element.22), calls=%async_computation.3 | async-start | bytes 9437184 | tf_op jit(solution)/shard_map/all_to_all | solution.py:265
  158.6 4.7 %copy-start.19 = (bf16[1024,512]{1,0:T(8,128)(2,1)S(1)}, bf16[1024,512]{1,0:T(8,128)(2,1)}, u32[]{:S(2)}) copy-start(bf16[1024,512]{1,0:T(8,128)(2,1)} %copy-done.18) | copy-start | bytes 3145732
  163.3 4.6 %copy-start.17 = (bf16[1024,512]{1,0:T(8,128)(2,1)S(1)}, bf16[1024,512]{1,0:T(8,128)(2,1)}, u32[]{:S(2)}) copy-start(bf16[1024,512]{1,0:T(8,128)(2,1)} %copy-done.16) | copy-start | bytes 3145732
  167.9 49.2 %copy-start.3 = (bf16[1,128,1152]{2,1,0:T(8,128)(2,1)S(1)}, bf16[1,128,1152]{2,1,0:T(8,128)(2,1)}, u32[]{:S(2)}) copy-start(bf16[1,128,1152]{2,1,0:T(8,128)(2,1)} %param.23) | copy-start | bytes 884740
  167.9 49.2 %copy-start.5 = (bf16[128,512]{1,0:T(8,128)(2,1)S(1)}, bf16[128,512]{1,0:T(8,128)(2,1)}, u32[]{:S(2)}) copy-start(bf16[128,512]{1,0:T(8,128)(2,1)} %copy-done.4) | copy-start | bytes 393220
  167.9 49.2 %copy-start.7 = (bf16[128,512]{1,0:T(8,128)(2,1)S(1)}, bf16[128,512]{1,0:T(8,128)(2,1)}, u32[]{:S(2)}) copy-start(bf16[128,512]{1,0:T(8,128)(2,1)} %copy-done.6) | copy-start | bytes 393220
  167.9 49.2 %copy-start.13 = (bf16[128,1152]{1,0:T(8,128)(2,1)S(1)}, bf16[128,1152]{1,0:T(8,128)(2,1)}, u32[]{:S(2)}) copy-start(bf16[128,1152]{1,0:T(8,128)(2,1)} %copy-done.12) | copy-start | bytes 884740

commit v2 on v0

v2 whole, which is shorter than its diff:
```python
import functools

import jax
import jax.numpy as jnp
from jax import lax
from jax.experimental import pallas as pl
from jax.experimental.pallas import tpu as pltpu
from jax.sharding import PartitionSpec as P

H = 16
F32 = jnp.float32
BF16 = jnp.bfloat16
WIDE = 640
STEP = 512
ROOMY = 60 * 1024 * 1024
SNUG = 32 * 1024 * 1024


def call(body, outs, cost, limit=SNUG, **extra):
    flops, moved = cost
    return pl.pallas_call(
        body,
        out_shape=outs,
        compiler_params=pltpu.CompilerParams(vmem_limit_bytes=limit),
        cost_estimate=pl.CostEstimate(flops=flops, bytes_accessed=moved, transcendentals=0),
        **extra,
    )


def shape(dims, dtype):
    return jax.ShapeDtypeStruct(dims, dtype)


def rows_of(blocks):
    n, eight, width = blocks.shape
    return blocks.astype(F32).reshape(n * eight, width)


def blocks_of(rows):
    total, width = rows.shape
    return rows.reshape(total // 8, 8, width).astype(BF16)


def pack_body(q_ref, k_ref, v_ref, out_ref):
    for s, ref in enumerate((q_ref, k_ref, v_ref)):
        for i in range(ref.shape[0]):
            for half in range(2):
                out_ref[i, half, 8 * s : 8 * s + 8, :] = ref[
                    i, :, STEP * half : STEP * half + WIDE
                ]


def iota(dims, axis):
    return lax.broadcasted_iota(jnp.int32, dims, axis)


def slot_lines(routes_ref, experts, cap):
    tok = routes_ref.shape[1]
    lines = [routes_ref[j : j + 1, :] for j in range(2)]
    onehots = [iota((experts, tok), 0) == line for line in lines]
    named = jnp.where(onehots[0] | onehots[1], 1.0, 0.0).astype(BF16)
    later = jnp.where(iota((tok, tok), 0) < iota((tok, tok), 1), 1.0, 0.0).astype(BF16)
    before = jnp.dot(named, later, preferred_element_type=F32)
    found = []
    for line, onehot in zip(lines, onehots):
        rank = jnp.sum(jnp.where(onehot, before, 0.0), axis=0, keepdims=True)
        place = (line & -4) | ((line & 1) << 1) | ((line >> 1) & 1)
        found.append((line.astype(F32), place.astype(F32) * cap + rank))
    return found


def slot_onehots(lines, slots):
    where = iota((slots, lines[0][1].shape[1]), 0).astype(F32)
    return [jnp.where(where == slot, 1.0, 0.0).astype(BF16) for _, slot in lines]


def expert_onehots(lines, experts):
    tok = lines[0][0].shape[1]
    diagonal = iota((tok, tok), 0) == iota((tok, tok), 1)
    found = []
    for expert, _ in lines:
        column = jnp.sum(jnp.where(diagonal, expert, 0.0), axis=1, keepdims=True)
        found.append(iota((tok, experts), 1) == column.astype(jnp.int32))
    return found


def attend_body(head_width, off_ref, qkv_ref, out_ref):
    frames = qkv_ref.shape[0]
    q, k, v = [rows_of(qkv_ref[:, 8 * s : 8 * s + 8, :]).astype(BF16) for s in range(3)]
    rows = frames * 8
    off = off_ref[0]
    same = (
        lax.broadcasted_iota(jnp.int32, (rows, rows), 0) & 7
    ) == (lax.broadcasted_iota(jnp.int32, (rows, rows), 1) & 7)
    lane = lax.broadcasted_iota(jnp.int32, (rows, 256), 1)
    tiles = [jnp.zeros((rows, 128), F32) for _ in range(WIDE // 128)]
    for h in range(H // 2):
        w = h // 2
        first = off + head_width * h - 128 * w
        inside = (lane >= first) & (lane < first + head_width)
        cols = slice(128 * w, 128 * w + 256)
        mine = jnp.where(inside, q[:, cols].astype(F32), 0.0).astype(BF16)
        scores = lax.dot_general(
            mine, k[:, cols], (((1,), (1,)), ((), ())), preferred_element_type=F32
        ) * head_width ** (-0.5)
        scores = jnp.where(same, scores, -1e30)
        peak = jnp.max(scores, axis=1, keepdims=True)
        weights = jnp.exp(scores - peak)
        probs = (weights / jnp.sum(weights, axis=1, keepdims=True)).astype(BF16)
        got = jnp.dot(probs, v[:, cols], preferred_element_type=F32)
        for t in range(2):
            part = slice(128 * t, 128 * t + 128)
            tiles[w + t] = jnp.where(inside[:, part], got[:, part], tiles[w + t])
    for t, tile in enumerate(tiles):
        out_ref[:, :, 128 * t : 128 * t + 128] = blocks_of(tile)


def inv_rms_of(hidden_float):
    return lax.rsqrt(jnp.mean(hidden_float * hidden_float, axis=-1, keepdims=True) + 1e-06)


def project_body(
    att_ref, residual_ref, w_out_ref, gain_ref, w_router_ref, routes_ref, cot_ref,
    hidden_ref, combine_ref, out_ref,
):
    low, high = rows_of(att_ref[:, 0]), rows_of(att_ref[:, 1])
    shared = WIDE - STEP
    attended = jnp.concatenate(
        [low[:, :STEP], low[:, STEP:] + high[:, :shared], high[:, shared:]], axis=1
    ).astype(BF16)
    stream = residual_ref[...].astype(F32) + jnp.dot(
        attended, w_out_ref[...], preferred_element_type=F32
    )
    hidden = stream.astype(BF16)
    hidden_ref[...] = hidden
    hidden_float = hidden.astype(F32)
    normed = (hidden_float * inv_rms_of(hidden_float) * gain_ref[...]).astype(BF16)
    chips, _, planes, cap, width = out_ref.shape
    experts = chips * planes
    lines = slot_lines(routes_ref, experts, cap)
    picks = slot_onehots(lines, experts * cap)
    picks = picks[0] + picks[1]
    step = 4
    for core, rows in enumerate((normed, cot_ref[...])):
        for at in range(0, chips, step):
            some = picks[at * planes * cap : (at + step) * planes * cap]
            blocks = blocks_of(jnp.dot(some, rows, preferred_element_type=F32))
            out_ref[at : at + step, core] = blocks.reshape(step, planes, cap, width)
    logits = jnp.dot(normed, w_router_ref[...], preferred_element_type=F32)
    for j, onehot in enumerate(expert_onehots(lines, experts)):
        chosen = jnp.sum(jnp.where(onehot, logits, 0.0), axis=1, keepdims=True)
        combine_ref[:, j : j + 1] = jax.nn.sigmoid(chosen)


def expert_body(
    state_ref, here_ref, there_ref, column_ref,
    home_gate_ref, home_up_ref, home_down_ref, new_gate_ref, new_up_ref, new_down_ref,
    keep_ref, send_ref, scaled_ref, units_ref, d_gate_ref, d_up_ref,
    gate_ref, up_ref, down_ref, sems,
):
    turned = (((1,), (1,)), ((), ()))
    first, moved = state_ref[0] == 0, state_ref[1] == 1
    opening = pl.program_id(0) == 0
    targets = (gate_ref, up_ref, down_ref)

    def fetch(sources):
        for n, (source, target) in enumerate(zip(sources, targets)):
            pltpu.make_async_copy(source, target, sems.at[n]).start()

    @pl.when(opening & moved)
    def _():
        fetch((new_gate_ref, new_up_ref, new_down_ref))

    @pl.when(opening & jnp.logical_not(moved))
    def _():
        fetch((home_gate_ref, home_up_ref, home_down_ref))

    def arrived(n):
        @pl.when(opening)
        def _():
            pltpu.make_async_copy(home_gate_ref if n < 2 else home_down_ref, targets[n],
                                  sems.at[n]).wait()

    def work(rows_ref, cot_ref, out_ref, in_ref):
        x = rows_ref[...]
        arrived(0)
        pre_gate = jnp.dot(x, gate_ref[0], preferred_element_type=F32)
        arrived(1)
        pre_up = jnp.dot(x, up_ref[0], preferred_element_type=F32)
        gate_sig = jax.nn.sigmoid(pre_gate)
        gate_act = pre_gate * gate_sig
        units = (gate_act * pre_up).astype(BF16)
        units_ref[...] = units
        arrived(2)
        out_ref[...] = jnp.dot(units, down_ref[0], preferred_element_type=F32).astype(BF16)
        chosen = jnp.sum(x.astype(F32) * column_ref[...], axis=1, keepdims=True)
        scaled = (jax.nn.sigmoid(chosen) * cot_ref[...].astype(F32)).astype(BF16)
        scaled_ref[...] = scaled
        d_units = lax.dot_general(scaled, down_ref[0], turned, preferred_element_type=F32)
        slope = pre_up * (gate_sig + gate_act * (1.0 - gate_sig))
        d_pre_gate = (d_units * slope).astype(BF16)
        d_pre_up = (d_units * gate_act).astype(BF16)
        d_gate_ref[...] = d_pre_gate
        d_up_ref[...] = d_pre_up
        in_ref[...] = (
            lax.dot_general(d_pre_gate, gate_ref[0], turned, preferred_element_type=F32)
            + lax.dot_general(d_pre_up, up_ref[0], turned, preferred_element_type=F32)
        ).astype(BF16)

    @pl.when(first)
    def _():
        work(here_ref, there_ref, keep_ref, send_ref)

    @pl.when(jnp.logical_not(first))
    def _():
        work(there_ref, here_ref, send_ref, keep_ref)


def down_body(units_ref, scaled_ref, out_ref):
    out_ref[0] = lax.dot_general(
        units_ref[...], scaled_ref[...], (((0,), (0,)), ((), ())), preferred_element_type=F32
    ).astype(BF16)


def gates_body(state_ref, here_ref, there_ref, left_ref, right_ref, gate_ref, up_ref):
    def work(x_ref):
        for ref, out_ref in ((left_ref, gate_ref), (right_ref, up_ref)):
            out_ref[0] = lax.dot_general(
                x_ref[...], ref[...], (((0,), (0,)), ((), ())), preferred_element_type=F32
            ).astype(BF16)

    for core, x_ref in enumerate((here_ref, there_ref)):
        pl.when(state_ref[0] == core)(functools.partial(work, x_ref))


def widen_body(state_ref, home_ref, new_ref, out_ref):
    out_ref[...] = jnp.where(state_ref[1] == 1, new_ref[...], home_ref[...]).astype(F32)


def spread(onehot, rows):
    return lax.dot_general(onehot, rows, (((0,), (0,)), ((), ())), preferred_element_type=F32)


def finish_body(
    back_ref, routes_ref, combine_ref, cot_ref, hidden_ref, gain_ref, w_router_ref,
    block_ref, d_hidden_ref, got_ref,
):
    chips, _, planes, cap, width = back_ref.shape
    experts = chips * planes
    tok = hidden_ref.shape[0]
    lines = slot_lines(routes_ref, experts, cap)
    picks = slot_onehots(lines, experts * cap)
    either = picks[0] + picks[1]
    combines = [combine_ref[:, j : j + 1] for j in range(2)]
    d_combines = [jnp.zeros((tok, 1), F32) for _ in range(2)]
    for at in range(0, width, 384):
        cols = slice(at, at + 384)
        outs, ins = [
            rows_of(back_ref[:, core, :, :, cols].reshape(experts, cap, 384)).astype(BF16)
            for core in range(2)
        ]
        got_ref[:, cols] = spread(either, ins)
        cotangent = cot_ref[:, cols].astype(F32)
        block = hidden_ref[:, cols].astype(F32)
        for j in range(2):
            expert_out = spread(picks[j], outs)
            block = block + combines[j] * expert_out
            d_combines[j] = d_combines[j] + jnp.sum(
                cotangent * expert_out, axis=1, keepdims=True
            )
        block_ref[:, cols] = block.astype(BF16)
    rows = jnp.zeros((tok, experts), F32)
    for j, onehot in enumerate(expert_onehots(lines, experts)):
        d_logit = d_combines[j] * combines[j] * (1.0 - combines[j])
        rows = rows + jnp.where(onehot, d_logit, 0.0)
    d_normed = got_ref[...] + lax.dot_general(
        rows,
        w_router_ref[...].astype(F32),
        (((1,), (1,)), ((), ())),
        precision=lax.Precision.HIGHEST,
        preferred_element_type=F32,
    )
    hidden_float = hidden_ref[...].astype(F32)
    inv_rms = inv_rms_of(hidden_float)
    gained = d_normed * gain_ref[...]
    d_norm_in = inv_rms * gained - hidden_float * inv_rms**3 * jnp.mean(
        gained * hidden_float, axis=-1, keepdims=True
    )
    d_hidden_ref[...] = (cot_ref[...].astype(F32) + d_norm_in).astype(BF16)


def relay(parcel, axes):
    return lax.all_to_all(parcel, axes, split_axis=0, concat_axis=0, tiled=True)


def on_device(
    residual, queries, keys_in, values, w_out, norm_gain, w_router, routes, w_gate, w_up, w_down,
    d_out,
):
    everyone = ("frames", "expert")
    frames = lax.axis_size("frames")
    planes = lax.axis_size("expert")
    devices = frames * planes
    chips = frames // 2
    width = residual.shape[2]
    tok = residual.shape[0] * residual.shape[1]
    experts = w_router.shape[1]
    cap = 4 * tok // experts
    slots = experts * cap
    hidden_units = w_gate.shape[2]
    smem = pl.BlockSpec(memory_space=pltpu.SMEM)
    fixed = lambda *dims: pl.BlockSpec(dims, lambda i: (0,) * len(dims))
    whole = lambda a: fixed(*a.shape)
    flat = lambda a: a.reshape(tok, width)
    eights = lambda a: a.reshape(tok // 8, 8, width)
    cot = flat(d_out)
    pairs = jnp.swapaxes(routes.reshape(tok, 2), 0, 1)
    gain = norm_gain.reshape(1, width)
    me, plane = lax.axis_index("frames"), lax.axis_index("expert")
    core = me % 2
    offset = (core * (width // 2 - STEP)).reshape(1)
    mine = 4 * (me // 2) + 2 * (plane % 2) + plane // 2
    column = lax.dynamic_slice(w_router, (0, mine), (width, 1)).astype(F32).reshape(1, width)
    swaps = [
        (f * planes + z, (f ^ 1) * planes + (z ^ 1))
        for f in range(frames)
        for z in range(planes)
        if (f + z) % 2
    ]
    state = jnp.stack([core, (me + plane) % 2]).astype(jnp.int32)
    swap = lambda a: lax.ppermute(a, everyone, swaps)
    beside = lambda a: lax.ppermute(a, "frames", [(i, i ^ 1) for i in range(frames)])

    moved_w = [swap(w) for w in (w_gate, w_up, w_down)]
    part = tok // 32
    packed = call(
        pack_body,
        shape((chips, 2, 24, WIDE), BF16),
        (0, 2 * frames * 24 * WIDE * 2),
        limit=ROOMY,
        grid=(4,),
        in_specs=[pl.BlockSpec((part, 8, width), lambda i: (i, 0, 0))] * 3,
        out_specs=pl.BlockSpec((part, 2, 24, WIDE), lambda i: (i, 0, 0, 0)),
    )(eights(queries), eights(keys_in), eights(values))
    qkv = relay(packed.reshape(frames, 24, WIDE), "frames")
    attended = call(
        lambda *refs: attend_body(width // H, *refs),
        shape((frames, 8, WIDE), BF16),
        (1 << 29, 4 * frames * 8 * WIDE * 2),
        grid=(1,),
        in_specs=[smem, fixed(frames, 24, WIDE)],
        out_specs=fixed(frames, 8, WIDE),
    )(offset, qkv)
    attended = relay(attended, "frames").reshape(chips, 2, 8, WIDE)
    hidden, combine, outbound = call(
        project_body,
        (shape((tok, width), BF16), shape((tok, 2), F32),
         shape((chips, 2, planes, cap, width), BF16)),
        (2 * tok * width * (width + 2 * slots), (width + 3 * slots) * width * 2),
        grid=(1,),
        in_specs=[whole(attended), whole(cot), whole(w_out), whole(gain), whole(w_router),
                  whole(pairs), whole(cot)],
        out_specs=(whole(cot), fixed(tok, 2), fixed(chips, 2, planes, cap, width)),
    )(attended, flat(residual), w_out, gain, w_router, pairs, cot)
    outbound, *moved_w = lax.optimization_barrier((outbound, *moved_w))
    here = relay(outbound.reshape(devices, cap, width), everyone)
    there = beside(here)

    total = devices * cap
    block = 512
    by_rows = lambda w: pl.BlockSpec((block, w), lambda i: (i, 0))
    rows = lambda a: a.reshape(total, width)
    product = 2 * total * width * hidden_units
    wide = shape((total, width), BF16)
    inner = shape((total, hidden_units), BF16)
    hbm = pl.BlockSpec(memory_space=pltpu.HBM)
    keep, send, scaled, units, d_pre_gate, d_pre_up = call(
        expert_body,
        (wide, wide, wide, inner, inner, inner),
        (6 * product, 10 * total * width * 2),
        limit=ROOMY,
        grid=(total // block,),
        in_specs=[smem, by_rows(width), by_rows(width), whole(column)] + [hbm] * 6,
        out_specs=[by_rows(width)] * 3 + [by_rows(hidden_units)] * 3,
        scratch_shapes=[
            pltpu.VMEM(w_gate.shape, BF16),
            pltpu.VMEM(w_up.shape, BF16),
            pltpu.VMEM(w_down.shape, BF16),
            pltpu.SemaphoreType.DMA((3,)),
        ],
    )(state, rows(here), rows(there), column, w_gate, w_up, w_down, *moved_w)
    got = beside(send)
    third = width // 3
    by_third = pl.BlockSpec((total, third), lambda i: (0, i))
    d_down = call(
        down_body,
        shape(w_down.shape, BF16),
        (product, 2 * total * width * 2),
        limit=ROOMY,
        grid=(3,),
        in_specs=[whole(units), by_third],
        out_specs=pl.BlockSpec((1, hidden_units, third), lambda i: (0, 0, i)),
    )(units, scaled)
    got, d_down = lax.optimization_barrier((got, d_down))
    returned = (keep.astype(F32) + got.astype(F32)).astype(BF16)
    back = relay(returned.reshape(devices, cap, width), everyone)
    back = back.reshape(chips, 2, planes, cap, width)

    def chosen(core_index):
        return lambda i, state: (0, jnp.where(state[0] == core_index, i, 0))

    still = lambda i, state: (0, 0)
    d_gate, d_up = pl.pallas_call(
        gates_body,
        out_shape=(shape(w_gate.shape, BF16), shape(w_up.shape, BF16)),
        grid_spec=pltpu.PrefetchScalarGridSpec(
            num_scalar_prefetch=1,
            grid=(3,),
            in_specs=[
                pl.BlockSpec((total, third), chosen(0)),
                pl.BlockSpec((total, third), chosen(1)),
                pl.BlockSpec((total, hidden_units), still),
                pl.BlockSpec((total, hidden_units), still),
            ],
            out_specs=[pl.BlockSpec((1, third, hidden_units), lambda i, state: (0, i, 0))] * 2,
        ),
        compiler_params=pltpu.CompilerParams(vmem_limit_bytes=ROOMY),
        cost_estimate=pl.CostEstimate(
            flops=2 * product, bytes_accessed=4 * total * width * 2, transcendentals=0
        ),
    )(state, rows(here), rows(there), d_pre_gate, d_pre_up)

    def widen(home, new):
        _, height, across = home.shape
        part = height // 4
        pick = lambda n: lambda i, state: (0, jnp.where(state[1] == n, i, 0), 0)
        return pl.pallas_call(
            widen_body,
            out_shape=shape(home.shape, F32),
            grid_spec=pltpu.PrefetchScalarGridSpec(
                num_scalar_prefetch=1,
                grid=(4,),
                in_specs=[pl.BlockSpec((1, part, across), pick(n)) for n in range(2)],
                out_specs=pl.BlockSpec((1, part, across), lambda i, state: (0, i, 0)),
            ),
            compiler_params=pltpu.CompilerParams(vmem_limit_bytes=SNUG),
            cost_estimate=pl.CostEstimate(
                flops=height * across, bytes_accessed=6 * height * across, transcendentals=0
            ),
        )(state, home, new)

    new_down = swap(d_down)
    new_gate = swap(d_gate)
    d_up, new_down = lax.optimization_barrier((d_up, new_down))
    new_up = swap(d_up)
    block_out, d_hidden = call(
        finish_body,
        (shape((tok, width), BF16), shape((tok, width), BF16)),
        (6 * tok * width * slots, 4 * slots * width * 2),
        limit=ROOMY,
        grid=(1,),
        in_specs=[whole(back), whole(pairs), whole(combine), whole(cot), whole(hidden),
                  whole(gain), whole(w_router)],
        out_specs=(whole(cot), whole(cot)),
        scratch_shapes=[pltpu.VMEM((tok, width), F32)],
    )(back, pairs, combine, cot, hidden, gain, w_router)
    new_up, d_hidden = lax.optimization_barrier((new_up, d_hidden))
    d_down, d_gate, d_up = [
        widen(*pair) for pair in ((d_down, new_down), (d_gate, new_gate), (d_up, new_up))
    ]
    return (
        block_out.reshape(residual.shape),
        d_hidden.reshape(residual.shape),
        d_gate,
        d_up,
        d_down,
    )


def solution(mesh):
    tokens = P("frames", "expert", None)
    weights = P(("frames", "expert"), None, None)
    return jax.shard_map(
        on_device,
        mesh=mesh,
        in_specs=(tokens,) * 4
        + (P(), P(), P(), P("expert", "frames", None, None))
        + (weights,) * 3
        + (tokens,),
        out_specs=(tokens, tokens, weights, weights, weights),
        check_vma=False,
    )
```

time: 215 us -> 203 us (0.944)
  waiting for transfers between devices: 120 us -> 63.6 us
  blocking collectives: 0 us -> 43.3 us
  Pallas kernels: 32.4 us -> 48.7 us
  matrix products: 14.1 us -> 0 us
  local copies, waits for them, and re-layouts: 14 us -> 4.2 us
  other arithmetic: 0 us -> 5 us
  starting transfers between devices: 33.2 us -> 36.5 us
    all_to_all x6 -> x3, waiting for transfers between devices: 120 us -> 16.6 us  [relay(): return lax.all_to_all(parcel, axes, split_axis=0, concat_axis=0, tiled=True)]
    ppermute x0 -> x8, waiting for transfers between devices: none -> 47.1 us  [the longest x6 44 us: on_device(): swap = lambda a: lax.ppermute(a, everyone, swaps)]
    all_to_all x0 -> x1, blocking collectives: none -> 43.3 us  [relay(): return lax.all_to_all(parcel, axes, split_axis=0, concat_axis=0, tiled=True)]
    ppermute x0 -> x8, starting transfers between devices: none -> 18.8 us  [the longest x6 17.9 us: on_device(): swap = lambda a: lax.ppermute(a, everyone, swaps)]
    pallas_call x7 -> x9, Pallas kernels: 30.1 us -> 45.9 us  [the longest x1 16.1 us: on_device(): call(expert_body, (wide, wide, wide, inner, inner, inner), (6 * product,...]
    all_to_all x6 -> x3, starting transfers between devices: 33.2 us -> 17.6 us  [relay(): return lax.all_to_all(parcel, axes, split_axis=0, concat_axis=0, tiled=True)]
    dot_general x3 -> x0, matrix products: 14.1 us -> none  [the longest x1 5.03 us: on_device(): d_down = jnp.dot(units.T, scaled, preferred_element_type=F32)]
    unnamed x52 -> x35, local copies, waits for them, and re-layouts: 14 us -> 4.19 us
  transfers between devices with their start and end apart: 6 -> 11, of which waited for: 6 -> 7; matrix products, arithmetic and copies ran while one was open for 7% -> 1% of each run, Pallas kernels for 8% -> 13%
where the time goes in v2:
time: 203 us; the launch traced here: 202 us
  waiting for transfers between devices  63.6 us (31%)
  Pallas kernels  48.7 us (24%)
  blocking collectives  43.3 us (21%)
  starting transfers between devices  36.5 us (18%)
  other arithmetic  5 us (2%)
  local copies, waits for them, and re-layouts  4.2 us (2%)
    ppermute x6, waiting for transfers between devices, on_device(): swap = lambda a: lax.ppermute(a, everyone, swaps)  44 us
    all_to_all x1, blocking collectives, relay(): return lax.all_to_all(parcel, axes, split_axis=0, concat_axis=0, tiled=True)  43.3 us
    ppermute x6, starting transfers between devices, on_device(): swap = lambda a: lax.ppermute(a, everyone, swaps)  17.9 us
    all_to_all x3, starting transfers between devices, relay(): return lax.all_to_all(parcel, axes, split_axis=0, concat_axis=0, tiled=True)  17.6 us
    all_to_all x3, waiting for transfers between devices, relay(): return lax.all_to_all(parcel, axes, split_axis=0, concat_axis=0, tiled=True)  16.6 us
    pallas_call x1, Pallas kernels, on_device(): call(expert_body, (wide, wide, wide, inner, inner, inner), (6 * product,...  16.1 us
    pallas_call x3, Pallas kernels, widen(): pl.pallas_call(widen_body, out_shape=shape(home.shape, F32), grid_spec=pl...  7.43 us
    pallas_call x1, Pallas kernels, on_device(): pl.pallas_call(gates_body, out_shape=(shape(w_gate.shape, BF16), shape(w_...  7.12 us
  transfers between devices with their start and end apart: 11, of which 7 were waited for; matrix products, arithmetic and copies ran while one was open for 1% of the time, Pallas kernels for 13%

profile of v2, /device:TPU:1, one launch (start us, length us, event | category | flops | bytes accessed | tf_op | source)
XLA Modules:
  0.0 202.2 jit_solution(12447355942287865132)
XLA Ops:
  0.6 3.4 %shard_map.155 = bf16[16,2,24,640]{3,2,1,0:T(8,128)(2,1)} custom-call(bf16[16,8,1152]{2,1,0:T(8,128)(2,1)} %bitcast.34, bf16[16,8,1152]{2,1,0:T(8,128)(2,1)} %bitcast.35, bf16[16,8,1152]{2,1,0:T(8,128)(2,1)} %bitcast.36), custom_call_target="tpu_custom_call" | custom-call | bytes 1966080 | tf_op jit(solution)/shard_map/pallas_call | solution.py:336
  4.0 0.0 copy-start.16
  4.0 0.0 copy-start.15
  4.0 0.0 copy-start.12
  4.0 8.9 %all-to-all-start = ((bf16[32,24,640]{2,1,0:T(8,128)(2,1)}), bf16[32,24,640]{2,1,0:T(8,128)(2,1)}, u32[]{:S(2)}, u32[]{:S(2)}) async-start(bf16[32,24,640]{2,1,0:T(8,128)(2,1)} %bitcast.31), calls=%async_computation | async-start | bytes 1966080 | tf_op jit(solution)/shard_map/all_to_all | solution.py:293
  12.9 3.7 %collective-permute-start = (bf16[1,1152,512]{2,1,0:T(8,128)(2,1)}, bf16[1,1152,512]{2,1,0:T(8,128)(2,1)}, u32[]{:S(2)}, u32[]{:S(2)}) collective-permute-start(bf16[1,1152,512]{2,1,0:T(8,128)(2,1)} %home_gate_ref.1), channel_id=1, source_target_pairs={{1,4},{3,6},{4,1},{6,3},{9,12},{11,14},{12,9},{14,11},{17,20},{19,... | collective-permute-start | bytes 3538952 | tf_op jit(solution)/shard_map/ppermute | solution.py:331
  16.7 1.9 collective-permute-start.1
  18.6 3.6 %collective-permute-start.2 = (bf16[1,512,1152]{2,1,0:T(8,128)(2,1)}, bf16[1,512,1152]{2,1,0:T(8,128)(2,1)}, u32[]{:S(2)}, u32[]{:S(2)}) collective-permute-start(bf16[1,512,1152]{2,1,0:T(8,128)(2,1)} %home_down_ref.1), channel_id=1, source_target_pairs={{1,4},{3,6},{4,1},{6,3},{9,12},{11,14},{12,9},{14,11},{17,20},{19,... | collective-permute-start | bytes 3538952 | tf_op jit(solution)/shard_map/ppermute | solution.py:331
  22.3 7.2 %all-to-all-done.refs_1_ = bf16[32,24,640]{2,1,0:T(8,128)(2,1)} async-done(((bf16[32,24,640]{2,1,0:T(8,128)(2,1)}), bf16[32,24,640]{2,1,0:T(8,128)(2,1)}, u32[]{:S(2)}, u32[]{:S(2)}) %all-to-all-start) | async-done | bytes 983072 | tf_op jit(solution)/shard_map/all_to_all | solution.py:293
  29.5 2.8 %shard_map.156 = bf16[32,8,640]{2,1,0:T(8,128)(2,1)S(1)} custom-call(s32[1]{0:T(128)} %bitcast.2.refs_0_, bf16[32,24,640]{2,1,0:T(8,128)(2,1)} %all-to-all-done.refs_1_), custom_call_target="tpu_custom_call" | custom-call | flops 536870912 | bytes 1310720 | tf_op jit(solution)/shard_map/pallas_call | solution.py:346
  32.2 0.0 copy-start.6
  32.2 0.7 copy-done.6
  33.0 3.9 %all-to-all-start.1 = ((bf16[32,8,640]{2,1,0:T(8,128)(2,1)}), bf16[32,8,640]{2,1,0:T(8,128)(2,1)S(1)}, u32[]{:S(2)}, u32[]{:S(2)}) async-start(bf16[32,8,640]{2,1,0:T(8,128)(2,1)} %copy-done.6), calls=%async_computation.1 | async-start | bytes 655360 | tf_op jit(solution)/shard_map/all_to_all | solution.py:293
  36.9 0.0 copy-done.16
  36.9 0.0 copy-done.15
  36.9 0.0 copy-start.10
  36.9 0.2 copy.17.w_router_ref
  37.2 9.4 %all-to-all-done.1 = bf16[32,8,640]{2,1,0:T(8,128)(2,1)S(1)} async-done(((bf16[32,8,640]{2,1,0:T(8,128)(2,1)}), bf16[32,8,640]{2,1,0:T(8,128)(2,1)S(1)}, u32[]{:S(2)}, u32[]{:S(2)}) %all-to-all-start.1) | async-done | bytes 327712 | tf_op jit(solution)/shard_map/all_to_all | solution.py:293
  46.5 0.0 copy-done.1
  46.5 0.0 copy-done.12
  46.5 1.0 copy-done.5
  47.5 1.0 copy-done.8
  48.5 1.7 shard_map.157
  50.2 0.0 copy-start.7
  50.2 0.0 copy-start.9
  50.2 0.0 collective-permute-done.new_gate_ref
  50.2 0.0 collective-permute-done.1.new_up_ref
  50.2 5.9 %collective-permute-done.2.new_down_ref = bf16[1,512,1152]{2,1,0:T(8,128)(2,1)} collective-permute-done((bf16[1,512,1152]{2,1,0:T(8,128)(2,1)}, bf16[1,512,1152]{2,1,0:T(8,128)(2,1)}, u32[]{:S(2)}, u32[]{:S(2)}) %collective-permute-start.2) | collective-permute-done | bytes 1179680 | tf_op jit(solution)/shard_map/ppermute | solution.py:331
  56.2 43.3 %all_to_all.20 = bf16[128,8,1152]{2,1,0:T(8,128)(2,1)S(1)} all-to-all(bf16[128,8,1152]{2,1,0:T(8,128)(2,1)S(1)} %bitcast.24), channel_id=1, replica_groups=mesh['frames'=32,'expert'=4] {'frames','expert'}, dimensions={0} | all-to-all | bytes 4718592 | tf_op jit(solution)/shard_map/all_to_all | solution.py:293
  99.5 0.0 copy-done.10
  99.5 0.0 copy-done.2
  99.5 0.0 copy-done.7
  99.5 0.0 copy-done.9
  99.5 0.0 copy-start.14
  99.5 0.6 collective-permute-start.3
  100.1 0.8 pad_add_fusion.state_ref
  100.8 0.6 bitcast_convert_fusion.column_ref
  101.4 3.0 %collective-permute-done.3 = bf16[128,8,1152]{2,1,0:T(8,128)(2,1)} collective-permute-done((bf16[128,8,1152]{2,1,0:T(8,128)(2,1)S(1)}, bf16[128,8,1152]{2,1,0:T(8,128)(2,1)}, u32[]{:S(2)}, u32[]{:S(2)}) %collective-permute-start.3) | collective-permute-done | bytes 2359328 | tf_op jit(solution)/shard_map/ppermute | solution.py:332
  104.5 0.0 copy-done.14
  104.5 16.1 %shard_map.158 = (bf16[1024,1152]{1,0:T(8,128)(2,1)}, bf16[1024,1152]{1,0:T(8,128)(2,1)}, bf16[1024,1152]{1,0:T(8,128)(2,1)}, bf16[1024,512]{1,0:T(8,128)(2,1)},...) custom-call(s32[2]{0:T(128)} %pad_add_fusion.state_ref, bf16[1024,1152]{1,0:T(8,128)(2,1)} %bitcast.32, ...), custom_call_target="tpu_custom_call" | custom-call | flops 7247757312 | bytes 23592960 | tf_op jit(solution)/shard_map/pallas_call | solution.py:377
  120.6 0.0 copy-start.13
  120.6 0.4 collective-permute-start.4
  120.9 5.2 %shard_map.159.home_ref = bf16[1,512,1152]{2,1,0:T(8,128)(2,1)} custom-call(bf16[1024,512]{1,0:T(8,128)(2,1)} %get-tuple-element.35.units_ref, bf16[1024,1152]{1,0:T(8,128)(2,1)} %get-tuple-element.36.scaled_ref), custom_call_target="tpu_custom_call" | custom-call | flops 1207959552 | bytes 4718592 | tf_op jit(solution)/shard_map/pallas_call | solution.py:395
  126.2 0.0 collective-permute-done.4
  126.2 0.0 copy-done.13
  126.2 3.6 %fusion = bf16[128,8,1152]{2,1,0:T(8,128)(2,1)} fusion(bf16[1024,1152]{1,0:T(8,128)(2,1)} %collective-permute-done.4, bf16[1024,1152]{1,0:T(8,128)(2,1)S(1)} %copy-done.13), kind=kLoop, calls=%fused_computation.1 | loop fusion | flops 4718592 | bytes 7077888 | tf_op jit(solution)/shard_map/reshape | solution.py:406
  129.8 4.8 %all-to-all-start.3 = ((bf16[128,8,1152]{2,1,0:T(8,128)(2,1)}), bf16[128,8,1152]{2,1,0:T(8,128)(2,1)}, u32[]{:S(2)}, u32[]{:S(2)}) async-start(bf16[128,8,1152]{2,1,0:T(8,128)(2,1)} %fusion), calls=%async_computation.3 | async-start | bytes 4718592 | tf_op jit(solution)/shard_map/all_to_all | solution.py:293
  134.6 0.0 copy-done
  134.6 3.8 %collective-permute-start.5 = (bf16[1,512,1152]{2,1,0:T(8,128)(2,1)S(1)}, bf16[1,512,1152]{2,1,0:T(8,128)(2,1)S(1)}, u32[]{:S(2)}, u32[]{:S(2)}) collective-permute-start(bf16[1,512,1152]{2,1,0:T(8,128)(2,1)S(1)} %copy-done), channel_id=1, source_target_pairs={{1,4},{3,6},{4,1},{6,3},{9,12},{11,14},{12,9},{14,11},{17,20},{19,... | collective-permute-start | bytes 3538952 | tf_op jit(solution)/shard_map/ppermute | solution.py:331
  138.4 0.0 copy-start.11
  138.4 7.1 %shard_map.161 = (bf16[1,1152,512]{2,1,0:T(8,128)(2,1)}, bf16[1,1152,512]{2,1,0:T(8,128)(2,1)}) custom-call(s32[2]{0:T(128)} %pad_add_fusion.state_ref, bf16[1024,1152]{1,0:T(8,128)(2,1)} %bitcast.33, bf16[1024,1152]{1,0:T(8,128)(2,1)} %bitcast.14.there_ref, bf16[1024,512]{1,0:T(8,128)(2,1)} %get-tuple-element.41.left_ref, ...), custom_call_target="tpu_custom_call" | custom-call | flops 2415919104 | bytes 9437184 | tf_op jit(solution)/shard_map/pallas_call | solution.py:413
  145.6 2.1 %collective-permute-start.7 = (bf16[1,1152,512]{2,1,0:T(8,128)(2,1)}, bf16[1,1152,512]{2,1,0:T(8,128)(2,1)S(1)}, u32[]{:S(2)}, u32[]{:S(2)}) collective-permute-start(bf16[1,1152,512]{2,1,0:T(8,128)(2,1)} %get-tuple-element.48.home_ref), channel_id=1, source_target_pairs={{1,4},{3,6},{4,1},{6,3},{9,12},{11,14},{12,9},{14,11},{17,20},{19,... | collective-permute-start | bytes 3538952 | tf_op jit(solution)/shard_map/ppermute | solution.py:331
  147.7 26.7 %collective-permute-done.5.new_ref = bf16[1,512,1152]{2,1,0:T(8,128)(2,1)S(1)} collective-permute-done((bf16[1,512,1152]{2,1,0:T(8,128)(2,1)S(1)}, bf16[1,512,1152]{2,1,0:T(8,128)(2,1)S(1)}, u32[]{:S(2)}, u32[]{:S(2)}) %collective-permute-start.5) | collective-permute-done | bytes 1179680 | tf_op jit(solution)/shard_map/ppermute | solution.py:331
  174.4 2.7 %collective-permute-start.6 = (bf16[1,1152,512]{2,1,0:T(8,128)(2,1)}, bf16[1,1152,512]{2,1,0:T(8,128)(2,1)S(1)}, u32[]{:S(2)}, u32[]{:S(2)}) collective-permute-start(bf16[1,1152,512]{2,1,0:T(8,128)(2,1)} %get-tuple-element.45.home_ref), channel_id=1, source_target_pairs={{1,4},{3,6},{4,1},{6,3},{9,12},{11,14},{12,9},{14,11},{17,20},{19,... | collective-permute-start | bytes 3538952 | tf_op jit(solution)/shard_map/ppermute | solution.py:331
  177.1 9.9 %collective-permute-done.7.new_ref = bf16[1,1152,512]{2,1,0:T(8,128)(2,1)S(1)} collective-permute-done((bf16[1,1152,512]{2,1,0:T(8,128)(2,1)}, bf16[1,1152,512]{2,1,0:T(8,128)(2,1)S(1)}, u32[]{:S(2)}, u32[]{:S(2)}) %collective-permute-start.7) | collective-permute-done | bytes 1179680 | tf_op jit(solution)/shard_map/ppermute | solution.py:331
  187.1 0.0 copy-done.11
  187.1 1.3 copy-done.4
  188.3 2.5 %shard_map.162 = f32[1,1152,512]{2,1,0:T(8,128)} custom-call(s32[2]{0:T(128)S(1)} %copy-done.11, bf16[1,1152,512]{2,1,0:T(8,128)(2,1)S(1)} %copy-done.4, bf16[1,1152,512]{2,1,0:T(8,128)(2,1)S(1)} %collective-permute-done.7.new_ref), custom_call_target="tpu_custom_call" | custom-call | flops 589824 | bytes 3538944 | tf_op jit(solution)/shard_map/pallas_call | solution.py:437
  190.8 2.5 %shard_map.164 = f32[1,512,1152]{2,1,0:T(8,128)} custom-call(s32[2]{0:T(128)S(1)} %copy-done.11, bf16[1,512,1152]{2,1,0:T(8,128)(2,1)S(1)} %copy-done, bf16[1,512,1152]{2,1,0:T(8,128)(2,1)S(1)} %collective-permute-done.5.new_ref), custom_call_target="tpu_custom_call" | custom-call | flops 589824 | bytes 3538944 | tf_op jit(solution)/shard_map/pallas_call | solution.py:437
  193.3 0.0 all-to-all-done.3
  193.3 5.0 %shard_map.160 = (bf16[128,1152]{1,0:T(8,128)(2,1)}, bf16[128,1152]{1,0:T(8,128)(2,1)}) custom-call(bf16[16,2,4,8,1152]{4,3,2,1,0:T(8,128)(2,1)} %bitcast.17.back_ref, s32[2,128]{1,0:T(2,128)} %bitcast.29, f32[128,2]{1,0:T(8,128)} %copy-done.9, bf16[128,1152]{1,0:T(8,128)(2,1)} %bitcast.26, bf16[128,1152]{1,0:T(8,128)(2,1)} %copy-done.7, ...), custom_call_target="tpu_custom_call" | custom-call | flops 452984832 | bytes 4718592 | tf_op jit(solution)/shard_map/pallas_call | solution.py:456
  198.3 1.4 collective-permute-done.6.new_ref
  199.7 0.0 copy-done.3
  199.7 2.5 %shard_map.163 = f32[1,1152,512]{2,1,0:T(8,128)} custom-call(s32[2]{0:T(128)S(1)} %copy-done.11, bf16[1,1152,512]{2,1,0:T(8,128)(2,1)S(1)} %copy-done.3, bf16[1,1152,512]{2,1,0:T(8,128)(2,1)S(1)} %collective-permute-done.6.new_ref), custom_call_target="tpu_custom_call" | custom-call | flops 589824 | bytes 3538944 | tf_op jit(solution)/shard_map/pallas_call | solution.py:437
  (8 shorter events, 0.0 us)
Async XLA Ops:
  4.0 32.9 %copy-start.16 = (f32[1152]{0:T(1024)S(1)}, f32[1152]{0:T(1024)}, u32[]{:S(2)}) copy-start(f32[1152]{0:T(1024)} %param.17) | copy-start | bytes 13828
  4.0 32.9 %copy-start.15 = (bf16[1152,64]{0,1:T(8,128)(2,1)S(1)}, bf16[1152,64]{0,1:T(8,128)(2,1)}, u32[]{:S(2)}) copy-start(bf16[1152,64]{0,1:T(8,128)(2,1)} %param.18) | copy-start | bytes 442372
  4.0 42.5 %copy-start.1 = (bf16[1152,1152]{1,0:T(8,128)(2,1)S(1)}, bf16[1152,1152]{1,0:T(8,128)(2,1)}, u32[]{:S(2)}) copy-start(bf16[1152,1152]{1,0:T(8,128)(2,1)} %w_out_ref.1) | copy-start | bytes 7962628
  4.0 42.5 %copy-start.12 = (s32[1,1,128,2]{2,3,1,0:T(2,128)S(1)}, s32[1,1,128,2]{2,3,1,0:T(2,128)}, u32[]{:S(2)}) copy-start(s32[1,1,128,2]{2,3,1,0:T(2,128)} %param.19) | copy-start | bytes 3076
  4.0 25.4 %all-to-all-start = ((bf16[32,24,640]{2,1,0:T(8,128)(2,1)}), bf16[32,24,640]{2,1,0:T(8,128)(2,1)}, u32[]{:S(2)}, u32[]{:S(2)}) async-start(bf16[32,24,640]{2,1,0:T(8,128)(2,1)} %bitcast.31), calls=%async_computation | async-start | bytes 1966080 | tf_op jit(solution)/shard_map/all_to_all | solution.py:293
  12.9 37.3 %collective-permute-start = (bf16[1,1152,512]{2,1,0:T(8,128)(2,1)}, bf16[1,1152,512]{2,1,0:T(8,128)(2,1)}, u32[]{:S(2)}, u32[]{:S(2)}) collective-permute-start(bf16[1,1152,512]{2,1,0:T(8,128)(2,1)} %home_gate_ref.1), channel_id=1, source_target_pairs={{1,4},{3,6},{4,1},{6,3},{9,12},{11,14},{12,9},{14,11},{17,20},{19,... | collective-permute-start | bytes 3538952 | tf_op jit(solution)/shard_map/ppermute | solution.py:331
  16.7 33.5 %collective-permute-start.1 = (bf16[1,1152,512]{2,1,0:T(8,128)(2,1)}, bf16[1,1152,512]{2,1,0:T(8,128)(2,1)}, u32[]{:S(2)}, u32[]{:S(2)}) collective-permute-start(bf16[1,1152,512]{2,1,0:T(8,128)(2,1)} %home_up_ref.1), channel_id=1, source_target_pairs={{1,4},{3,6},{4,1},{6,3},{9,12},{11,14},{12,9},{14,11},{17,20},{19,... | collective-permute-start | bytes 3538952 | tf_op jit(solution)/shard_map/ppermute | solution.py:331
  18.6 37.5 %collective-permute-start.2 = (bf16[1,512,1152]{2,1,0:T(8,128)(2,1)}, bf16[1,512,1152]{2,1,0:T(8,128)(2,1)}, u32[]{:S(2)}, u32[]{:S(2)}) collective-permute-start(bf16[1,512,1152]{2,1,0:T(8,128)(2,1)} %home_down_ref.1), channel_id=1, source_target_pairs={{1,4},{3,6},{4,1},{6,3},{9,12},{11,14},{12,9},{14,11},{17,20},{19,... | collective-permute-start | bytes 3538952 | tf_op jit(solution)/shard_map/ppermute | solution.py:331
  32.2 0.7 copy-start.6
  33.0 13.6 %all-to-all-start.1 = ((bf16[32,8,640]{2,1,0:T(8,128)(2,1)}), bf16[32,8,640]{2,1,0:T(8,128)(2,1)S(1)}, u32[]{:S(2)}, u32[]{:S(2)}) async-start(bf16[32,8,640]{2,1,0:T(8,128)(2,1)} %copy-done.6), calls=%async_computation.1 | async-start | bytes 655360 | tf_op jit(solution)/shard_map/all_to_all | solution.py:293
  36.9 62.6 %copy-start.10 = (f32[1,1152]{1,0:T(1,128)}, f32[1,1152]{1,0:T(1,128)S(1)}, u32[]{:S(2)}) copy-start(f32[1,1152]{1,0:T(1,128)S(1)} %reshape.75.gain_ref) | copy-start | bytes 13828
  37.2 62.4 %copy-start.2 = (bf16[1152,64]{1,0:T(8,128)(2,1)}, bf16[1152,64]{1,0:T(8,128)(2,1)S(1)}, u32[]{:S(2)}) copy-start(bf16[1152,64]{1,0:T(8,128)(2,1)S(1)} %copy.17.w_router_ref) | copy-start | bytes 442372
  46.5 1.0 copy-start.5
  47.5 1.0 copy-start.8
  50.2 49.3 %copy-start.7 = (bf16[128,1152]{1,0:T(8,128)(2,1)}, bf16[128,1152]{1,0:T(8,128)(2,1)S(1)}, u32[]{:S(2)}) copy-start(bf16[128,1152]{1,0:T(8,128)(2,1)S(1)} %get-tuple-element.39.hidden_ref) | copy-start | bytes 884740
  50.2 49.3 %copy-start.9 = (f32[128,2]{1,0:T(8,128)}, f32[128,2]{1,0:T(8,128)S(1)}, u32[]{:S(2)}) copy-start(f32[128,2]{1,0:T(8,128)S(1)} %get-tuple-element.38.combine_ref) | copy-start | bytes 3076
  99.5 4.9 %copy-start.14 = (bf16[128,8,1152]{2,1,0:T(8,128)(2,1)}, bf16[128,8,1152]{2,1,0:T(8,128)(2,1)S(1)}, u32[]{:S(2)}) copy-start(bf16[128,8,1152]{2,1,0:T(8,128)(2,1)S(1)} %all_to_all.20) | copy-start | bytes 7077892
  99.5 4.9 %collective-permute-start.3 = (bf16[128,8,1152]{2,1,0:T(8,128)(2,1)S(1)}, bf16[128,8,1152]{2,1,0:T(8,128)(2,1)}, u32[]{:S(2)}, u32[]{:S(2)}) collective-permute-start(bf16[128,8,1152]{2,1,0:T(8,128)(2,1)S(1)} %all_to_all.20), channel_id=1, source_target_pairs={{0,4},{4,0},{8,12},{12,8},{16,20},{20,16},{24,28},{28,24},{32,36},... | collective-permute-start | bytes 7077896 | tf_op jit(solution)/shard_map/ppermute | solution.py:332
  120.6 5.6 %copy-start.13 = (bf16[1024,1152]{1,0:T(8,128)(2,1)S(1)}, bf16[1024,1152]{1,0:T(8,128)(2,1)}, u32[]{:S(2)}) copy-start(bf16[1024,1152]{1,0:T(8,128)(2,1)} %get-tuple-element.33) | copy-start | bytes 7077892
  120.6 5.6 %collective-permute-start.4 = (bf16[1024,1152]{1,0:T(8,128)(2,1)}, bf16[1024,1152]{1,0:T(8,128)(2,1)}, u32[]{:S(2)}, u32[]{:S(2)}) collective-permute-start(bf16[1024,1152]{1,0:T(8,128)(2,1)} %get-tuple-element.34), channel_id=1, source_target_pairs={{0,4},{4,0},{8,12},{12,8},{16,20},{20,16},{24,28},{28,24},{32,36},... | collective-permute-start | bytes 7077896 | tf_op jit(solution)/shard_map/ppermute | solution.py:332
  129.8 4.8 %copy-start = (bf16[1,512,1152]{2,1,0:T(8,128)(2,1)S(1)}, bf16[1,512,1152]{2,1,0:T(8,128)(2,1)}, u32[]{:S(2)}) copy-start(bf16[1,512,1152]{2,1,0:T(8,128)(2,1)} %shard_map.159.home_ref) | copy-start | bytes 3538948
  129.8 63.5 %all-to-all-start.3 = ((bf16[128,8,1152]{2,1,0:T(8,128)(2,1)}), bf16[128,8,1152]{2,1,0:T(8,128)(2,1)}, u32[]{:S(2)}, u32[]{:S(2)}) async-start(bf16[128,8,1152]{2,1,0:T(8,128)(2,1)} %fusion), calls=%async_computation.3 | async-start | bytes 4718592 | tf_op jit(solution)/shard_map/all_to_all | solution.py:293
  134.6 39.8 %collective-permute-start.5 = (bf16[1,512,1152]{2,1,0:T(8,128)(2,1)S(1)}, bf16[1,512,1152]{2,1,0:T(8,128)(2,1)S(1)}, u32[]{:S(2)}, u32[]{:S(2)}) collective-permute-start(bf16[1,512,1152]{2,1,0:T(8,128)(2,1)S(1)} %copy-done), channel_id=1, source_target_pairs={{1,4},{3,6},{4,1},{6,3},{9,12},{11,14},{12,9},{14,11},{17,20},{19,... | collective-permute-start | bytes 3538952 | tf_op jit(solution)/shard_map/ppermute | solution.py:331
  138.4 48.6 %copy-start.11 = (s32[2]{0:T(128)S(1)}, s32[2]{0:T(128)}, u32[]{:S(2)}) copy-start(s32[2]{0:T(128)} %pad_add_fusion.state_ref) | copy-start | bytes 28
  145.6 41.5 %collective-permute-start.7 = (bf16[1,1152,512]{2,1,0:T(8,128)(2,1)}, bf16[1,1152,512]{2,1,0:T(8,128)(2,1)S(1)}, u32[]{:S(2)}, u32[]{:S(2)}) collective-permute-start(bf16[1,1152,512]{2,1,0:T(8,128)(2,1)} %get-tuple-element.48.home_ref), channel_id=1, source_target_pairs={{1,4},{3,6},{4,1},{6,3},{9,12},{11,14},{12,9},{14,11},{17,20},{19,... | collective-permute-start | bytes 3538952 | tf_op jit(solution)/shard_map/ppermute | solution.py:331
  174.4 25.3 %collective-permute-start.6 = (bf16[1,1152,512]{2,1,0:T(8,128)(2,1)}, bf16[1,1152,512]{2,1,0:T(8,128)(2,1)S(1)}, u32[]{:S(2)}, u32[]{:S(2)}) collective-permute-start(bf16[1,1152,512]{2,1,0:T(8,128)(2,1)} %get-tuple-element.45.home_ref), channel_id=1, source_target_pairs={{1,4},{3,6},{4,1},{6,3},{9,12},{11,14},{12,9},{14,11},{17,20},{19,... | collective-permute-start | bytes 3538952 | tf_op jit(solution)/shard_map/ppermute | solution.py:331
  187.1 1.3 copy-start.4
  193.3 6.4 %copy-start.3 = (bf16[1,1152,512]{2,1,0:T(8,128)(2,1)S(1)}, bf16[1,1152,512]{2,1,0:T(8,128)(2,1)}, u32[]{:S(2)}) copy-start(bf16[1,1152,512]{2,1,0:T(8,128)(2,1)} %get-tuple-element.45.home_ref) | copy-start | bytes 3538948

commit v3 on v2

--- a/solution.py
+++ b/solution.py
@@ -391,18 +391,25 @@
     )(state, rows(here), rows(there), column, w_gate, w_up, w_down, *moved_w)
     got = beside(send)
     third = width // 3
-    by_third = pl.BlockSpec((total, third), lambda i: (0, i))
-    d_down = call(
-        down_body,
-        shape(w_down.shape, BF16),
-        (product, 2 * total * width * 2),
-        limit=ROOMY,
-        grid=(3,),
-        in_specs=[whole(units), by_third],
-        out_specs=pl.BlockSpec((1, hidden_units, third), lambda i: (0, 0, i)),
-    )(units, scaled)
-    got, d_down = lax.optimization_barrier((got, d_down))
+    half = hidden_units // 2
+
+    def down_rows(n):
+        return call(
+            down_body,
+            shape((1, half, width), BF16),
+            (product // 2, 2 * total * width * 2),
+            limit=ROOMY,
+            grid=(1,),
+            in_specs=[pl.BlockSpec((total, half), lambda i: (0, n)), whole(scaled)],
+            out_specs=fixed(1, half, width),
+        )(units, scaled)
+
+    upper = down_rows(0)
+    new_upper = swap(upper)
+    lower = down_rows(1)
+    got, lower = lax.optimization_barrier((got, lower))
     returned = (keep.astype(F32) + got.astype(F32)).astype(BF16)
+    returned, new_upper = lax.optimization_barrier((returned, new_upper))
     back = relay(returned.reshape(devices, cap, width), everyone)
     back = back.reshape(chips, 2, planes, cap, width)
 
@@ -449,9 +456,9 @@
             ),
         )(state, home, new)
 
-    new_down = swap(d_down)
+    new_lower = swap(lower)
     new_gate = swap(d_gate)
-    d_up, new_down = lax.optimization_barrier((d_up, new_down))
+    d_up, new_lower = lax.optimization_barrier((d_up, new_lower))
     new_up = swap(d_up)
     block_out, d_hidden = call(
         finish_body,
@@ -465,9 +472,13 @@
         scratch_shapes=[pltpu.VMEM((tok, width), F32)],
     )(back, pairs, combine, cot, hidden, gain, w_router)
     new_up, d_hidden = lax.optimization_barrier((new_up, d_hidden))
-    d_down, d_gate, d_up = [
-        widen(*pair) for pair in ((d_down, new_down), (d_gate, new_gate), (d_up, new_up))
+    upper, lower, d_gate, d_up = [
+        widen(*pair)
+        for pair in (
+            (upper, new_upper), (lower, new_lower), (d_gate, new_gate), (d_up, new_up)
+        )
     ]
+    d_down = jnp.concatenate([upper, lower], axis=1)
     return (
         block_out.reshape(residual.shape),
         d_hidden.reshape(residual.shape),

time: 203 us -> 202 us (level)
  waiting for transfers between devices: 63.6 us -> 56.9 us
  starting transfers between devices: 36.5 us -> 39.6 us
    ppermute x6 -> x7, waiting for transfers between devices: 44 us -> 37.3 us  [on_device(): swap = lambda a: lax.ppermute(a, everyone, swaps)]
    convert_element_type x0 -> x1, other arithmetic: none -> 3.65 us  [on_device(): returned = (keep.astype(F32) + got.astype(F32)).astype(BF16)]
    reshape x1 -> x0, other arithmetic: 3.65 us -> none  [on_device(): back = relay(returned.reshape(devices, cap, width), everyone)]
    ppermute x6 -> x7, starting transfers between devices: 17.9 us -> 21.1 us  [on_device(): swap = lambda a: lax.ppermute(a, everyone, swaps)]
    pallas_call x1 -> x2, Pallas kernels: 5.24 us -> 7.14 us  [down_rows(): call(down_body, shape((1, half, width), BF16), (product // 2, 2 * total *...]
    pallas_call x3 -> x4, Pallas kernels: 7.43 us -> 6.4 us  [widen(): pl.pallas_call(widen_body, out_shape=shape(home.shape, F32), grid_spec=pl...]
    unnamed x35 -> x37, local copies, waits for them, and re-layouts: 4.19 us -> 4.21 us
  transfers between devices with their start and end apart: 11 -> 12, of which waited for: 7 -> 8; matrix products, arithmetic and copies ran while one was open for 1% -> 3% of each run, Pallas kernels for 13% -> 14%
where the time goes in v3:
time: 202 us; the launch traced here: 201 us
  waiting for transfers between devices  56.9 us (28%)
  Pallas kernels  49.5 us (25%)
  blocking collectives  43.3 us (21%)
  starting transfers between devices  39.6 us (20%)
  other arithmetic  6.5 us (3%)
  local copies, waits for them, and re-layouts  4.21 us (2%)
    all_to_all x1, blocking collectives, relay(): return lax.all_to_all(parcel, axes, split_axis=0, concat_axis=0, tiled=True)  43.3 us
    ppermute x7, waiting for transfers between devices, on_device(): swap = lambda a: lax.ppermute(a, everyone, swaps)  37.3 us
    ppermute x7, starting transfers between devices, on_device(): swap = lambda a: lax.ppermute(a, everyone, swaps)  21.1 us
    all_to_all x3, starting transfers between devices, relay(): return lax.all_to_all(parcel, axes, split_axis=0, concat_axis=0, tiled=True)  17.6 us
    all_to_all x3, waiting for transfers between devices, relay(): return lax.all_to_all(parcel, axes, split_axis=0, concat_axis=0, tiled=True)  16.5 us
    pallas_call x1, Pallas kernels, on_device(): call(expert_body, (wide, wide, wide, inner, inner, inner), (6 * product,...  16.1 us
    pallas_call x2, Pallas kernels, down_rows(): call(down_body, shape((1, half, width), BF16), (product // 2, 2 * total *...  7.14 us
    pallas_call x1, Pallas kernels, on_device(): pl.pallas_call(gates_body, out_shape=(shape(w_gate.shape, BF16), shape(w_...  7.12 us
  transfers between devices with their start and end apart: 12, of which 8 were waited for; matrix products, arithmetic and copies ran while one was open for 3% of the time, Pallas kernels for 14%

profile of v3, /device:TPU:1, one launch (start us, length us, event | category | flops | bytes accessed | tf_op | source)
XLA Modules:
  0.0 201.0 jit_solution(14895583515164066795)
XLA Ops:
  0.6 3.4 %shard_map.155 = bf16[16,2,24,640]{3,2,1,0:T(8,128)(2,1)} custom-call(bf16[16,8,1152]{2,1,0:T(8,128)(2,1)} %bitcast.33, bf16[16,8,1152]{2,1,0:T(8,128)(2,1)} %bitcast.34, bf16[16,8,1152]{2,1,0:T(8,128)(2,1)} %bitcast.35), custom_call_target="tpu_custom_call" | custom-call | bytes 1966080 | tf_op jit(solution)/shard_map/pallas_call | solution.py:336
  4.0 0.0 copy-start.13
  4.0 8.9 %all-to-all-start = ((bf16[32,24,640]{2,1,0:T(8,128)(2,1)}), bf16[32,24,640]{2,1,0:T(8,128)(2,1)}, u32[]{:S(2)}, u32[]{:S(2)}) async-start(bf16[32,24,640]{2,1,0:T(8,128)(2,1)} %bitcast.30), calls=%async_computation | async-start | bytes 1966080 | tf_op jit(solution)/shard_map/all_to_all | solution.py:293
  12.9 3.7 %collective-permute-start = (bf16[1,1152,512]{2,1,0:T(8,128)(2,1)}, bf16[1,1152,512]{2,1,0:T(8,128)(2,1)}, u32[]{:S(2)}, u32[]{:S(2)}) collective-permute-start(bf16[1,1152,512]{2,1,0:T(8,128)(2,1)} %home_gate_ref.1), channel_id=1, source_target_pairs={{1,4},{3,6},{4,1},{6,3},{9,12},{11,14},{12,9},{14,11},{17,20},{19,... | collective-permute-start | bytes 3538952 | tf_op jit(solution)/shard_map/ppermute | solution.py:331
  16.7 1.9 collective-permute-start.1
  18.6 3.6 %collective-permute-start.2 = (bf16[1,512,1152]{2,1,0:T(8,128)(2,1)}, bf16[1,512,1152]{2,1,0:T(8,128)(2,1)}, u32[]{:S(2)}, u32[]{:S(2)}) collective-permute-start(bf16[1,512,1152]{2,1,0:T(8,128)(2,1)} %home_down_ref.1), channel_id=1, source_target_pairs={{1,4},{3,6},{4,1},{6,3},{9,12},{11,14},{12,9},{14,11},{17,20},{19,... | collective-permute-start | bytes 3538952 | tf_op jit(solution)/shard_map/ppermute | solution.py:331
  22.3 7.2 %all-to-all-done.refs_1_ = bf16[32,24,640]{2,1,0:T(8,128)(2,1)} async-done(((bf16[32,24,640]{2,1,0:T(8,128)(2,1)}), bf16[32,24,640]{2,1,0:T(8,128)(2,1)}, u32[]{:S(2)}, u32[]{:S(2)}) %all-to-all-start) | async-done | bytes 983072 | tf_op jit(solution)/shard_map/all_to_all | solution.py:293
  29.5 2.8 %shard_map.156 = bf16[32,8,640]{2,1,0:T(8,128)(2,1)S(1)} custom-call(s32[1]{0:T(128)} %bitcast.2.refs_0_, bf16[32,24,640]{2,1,0:T(8,128)(2,1)} %all-to-all-done.refs_1_), custom_call_target="tpu_custom_call" | custom-call | flops 536870912 | bytes 1310720 | tf_op jit(solution)/shard_map/pallas_call | solution.py:346
  32.2 0.0 copy-start.7
  32.2 0.7 copy-done.7
  33.0 3.9 %all-to-all-start.1 = ((bf16[32,8,640]{2,1,0:T(8,128)(2,1)}), bf16[32,8,640]{2,1,0:T(8,128)(2,1)S(1)}, u32[]{:S(2)}, u32[]{:S(2)}) async-start(bf16[32,8,640]{2,1,0:T(8,128)(2,1)} %copy-done.7), calls=%async_computation.1 | async-start | bytes 655360 | tf_op jit(solution)/shard_map/all_to_all | solution.py:293
  36.9 0.0 copy-done.17
  36.9 0.0 copy-done.16
  36.9 0.0 copy-start.11
  36.9 0.2 copy.17.w_router_ref
  37.2 0.0 copy-start.1
  37.2 9.4 %all-to-all-done.1 = bf16[32,8,640]{2,1,0:T(8,128)(2,1)S(1)} async-done(((bf16[32,8,640]{2,1,0:T(8,128)(2,1)}), bf16[32,8,640]{2,1,0:T(8,128)(2,1)S(1)}, u32[]{:S(2)}, u32[]{:S(2)}) %all-to-all-start.1) | async-done | bytes 327712 | tf_op jit(solution)/shard_map/all_to_all | solution.py:293
  46.5 0.0 copy-done
  46.5 0.0 copy-done.13
  46.5 1.0 copy-done.6
  47.5 1.0 copy-done.9
  48.5 1.7 shard_map.157
  50.2 0.0 copy-start.8
  50.2 0.0 copy-start.10
  50.2 0.0 collective-permute-done.new_gate_ref
  50.2 0.0 collective-permute-done.1.new_up_ref
  50.2 5.9 %collective-permute-done.2.new_down_ref = bf16[1,512,1152]{2,1,0:T(8,128)(2,1)} collective-permute-done((bf16[1,512,1152]{2,1,0:T(8,128)(2,1)}, bf16[1,512,1152]{2,1,0:T(8,128)(2,1)}, u32[]{:S(2)}, u32[]{:S(2)}) %collective-permute-start.2) | collective-permute-done | bytes 1179680 | tf_op jit(solution)/shard_map/ppermute | solution.py:331
  56.2 43.3 %all_to_all.20 = bf16[128,8,1152]{2,1,0:T(8,128)(2,1)S(1)} all-to-all(bf16[128,8,1152]{2,1,0:T(8,128)(2,1)S(1)} %bitcast.23), channel_id=1, replica_groups=mesh['frames'=32,'expert'=4] {'frames','expert'}, dimensions={0} | all-to-all | bytes 4718592 | tf_op jit(solution)/shard_map/all_to_all | solution.py:293
  99.5 0.0 copy-done.11
  99.5 0.0 copy-done.1
  99.5 0.0 copy-done.8
  99.5 0.0 copy-done.10
  99.5 0.0 copy-start.15
  99.5 0.6 collective-permute-start.3
  100.1 0.7 pad_add_fusion.state_ref
  100.8 0.6 bitcast_convert_fusion.column_ref
  101.4 3.1 %collective-permute-done.3 = bf16[128,8,1152]{2,1,0:T(8,128)(2,1)} collective-permute-done((bf16[128,8,1152]{2,1,0:T(8,128)(2,1)S(1)}, bf16[128,8,1152]{2,1,0:T(8,128)(2,1)}, u32[]{:S(2)}, u32[]{:S(2)}) %collective-permute-start.3) | collective-permute-done | bytes 2359328 | tf_op jit(solution)/shard_map/ppermute | solution.py:332
  104.5 0.0 copy-done.15
  104.5 16.1 %shard_map.158 = (bf16[1024,1152]{1,0:T(8,128)(2,1)}, bf16[1024,1152]{1,0:T(8,128)(2,1)}, bf16[1024,1152]{1,0:T(8,128)(2,1)}, bf16[1024,512]{1,0:T(8,128)(2,1)},...) custom-call(s32[2]{0:T(128)} %pad_add_fusion.state_ref, bf16[1024,1152]{1,0:T(8,128)(2,1)} %bitcast.31, ...), custom_call_target="tpu_custom_call" | custom-call | flops 7247757312 | bytes 23592960 | tf_op jit(solution)/shard_map/pallas_call | solution.py:377
  120.5 0.4 collective-permute-start.4
  120.9 3.5 %shard_map.160.home_ref = bf16[1,256,1152]{2,1,0:T(8,128)(2,1)} custom-call(bf16[1024,512]{1,0:T(8,128)(2,1)} %get-tuple-element.37.units_ref, bf16[1024,1152]{1,0:T(8,128)(2,1)} %get-tuple-element.38.scaled_ref), custom_call_target="tpu_custom_call" | custom-call | flops 603979776 | bytes 4718592 | tf_op jit(solution)/shard_map/pallas_call | solution.py:397
  124.4 2.7 %collective-permute-start.5 = (bf16[1,256,1152]{2,1,0:T(8,128)(2,1)}, bf16[1,256,1152]{2,1,0:T(8,128)(2,1)S(1)}, u32[]{:S(2)}, u32[]{:S(2)}) collective-permute-start(bf16[1,256,1152]{2,1,0:T(8,128)(2,1)} %shard_map.160.home_ref), channel_id=1, source_target_pairs={{1,4},{3,6},{4,1},{6,3},{9,12},{11,14},{12,9},{14,11},{17,20},{19,... | collective-permute-start | bytes 1769480 | tf_op jit(solution)/shard_map/ppermute | solution.py:331
  127.1 3.6 %shard_map.159.home_ref = bf16[1,256,1152]{2,1,0:T(8,128)(2,1)} custom-call(bf16[1024,512]{1,0:T(8,128)(2,1)} %get-tuple-element.37.units_ref, bf16[1024,1152]{1,0:T(8,128)(2,1)} %get-tuple-element.38.scaled_ref), custom_call_target="tpu_custom_call" | custom-call | flops 603979776 | bytes 4718592 | tf_op jit(solution)/shard_map/pallas_call | solution.py:397
  130.7 0.0 collective-permute-done.4
  130.7 0.0 copy-done.14
  130.7 3.6 %add_convert_fusion = bf16[1024,1152]{1,0:T(8,128)(2,1)} fusion(bf16[1024,1152]{1,0:T(8,128)(2,1)} %collective-permute-done.4, bf16[1024,1152]{1,0:T(8,128)(2,1)S(1)} %copy-done.14), kind=kLoop, calls=%fused_computation | loop fusion | flops 4718592 | bytes 7077888 | tf_op jit(solution)/shard_map/convert_element_type | solution.py:411
  134.4 1.6 collective-permute-done.5.new_ref
  136.0 4.8 %all-to-all-start.3 = ((bf16[128,8,1152]{2,1,0:T(8,128)(2,1)}), bf16[128,8,1152]{2,1,0:T(8,128)(2,1)}, u32[]{:S(2)}, u32[]{:S(2)}) async-start(bf16[128,8,1152]{2,1,0:T(8,128)(2,1)} %bitcast.16), calls=%async_computation.3 | async-start | bytes 4718592 | tf_op jit(solution)/shard_map/all_to_all | solution.py:293
  140.8 3.0 %collective-permute-start.6 = (bf16[1,256,1152]{2,1,0:T(8,128)(2,1)S(1)}, bf16[1,256,1152]{2,1,0:T(8,128)(2,1)S(1)}, u32[]{:S(2)}, u32[]{:S(2)}) collective-permute-start(bf16[1,256,1152]{2,1,0:T(8,128)(2,1)S(1)} %copy-done.3), channel_id=1, source_target_pairs={{1,4},{3,6},{4,1},{6,3},{9,12},{11,14},{12,9},{14,11},{17,20},{19,... | collective-permute-start | bytes 1769480 | tf_op jit(solution)/shard_map/ppermute | solution.py:331
  143.8 7.1 %shard_map.162 = (bf16[1,1152,512]{2,1,0:T(8,128)(2,1)}, bf16[1,1152,512]{2,1,0:T(8,128)(2,1)}) custom-call(s32[2]{0:T(128)} %pad_add_fusion.state_ref, bf16[1024,1152]{1,0:T(8,128)(2,1)} %bitcast.32, bf16[1024,1152]{1,0:T(8,128)(2,1)} %bitcast.14.there_ref, bf16[1024,512]{1,0:T(8,128)(2,1)} %get-tuple-element.44.left_ref, ...), custom_call_target="tpu_custom_call" | custom-call | flops 2415919104 | bytes 9437184 | tf_op jit(solution)/shard_map/pallas_call | solution.py:420
  150.9 2.8 %collective-permute-start.8 = (bf16[1,1152,512]{2,1,0:T(8,128)(2,1)}, bf16[1,1152,512]{2,1,0:T(8,128)(2,1)S(1)}, u32[]{:S(2)}, u32[]{:S(2)}) collective-permute-start(bf16[1,1152,512]{2,1,0:T(8,128)(2,1)} %get-tuple-element.51.home_ref), channel_id=1, source_target_pairs={{1,4},{3,6},{4,1},{6,3},{9,12},{11,14},{12,9},{14,11},{17,20},{19,... | collective-permute-start | bytes 3538952 | tf_op jit(solution)/shard_map/ppermute | solution.py:331
  153.7 19.6 %collective-permute-done.6.new_ref = bf16[1,256,1152]{2,1,0:T(8,128)(2,1)S(1)} collective-permute-done((bf16[1,256,1152]{2,1,0:T(8,128)(2,1)S(1)}, bf16[1,256,1152]{2,1,0:T(8,128)(2,1)S(1)}, u32[]{:S(2)}, u32[]{:S(2)}) %collective-permute-start.6) | collective-permute-done | bytes 589856 | tf_op jit(solution)/shard_map/ppermute | solution.py:331
  173.3 3.3 %collective-permute-start.7 = (bf16[1,1152,512]{2,1,0:T(8,128)(2,1)}, bf16[1,1152,512]{2,1,0:T(8,128)(2,1)S(1)}, u32[]{:S(2)}, u32[]{:S(2)}) collective-permute-start(bf16[1,1152,512]{2,1,0:T(8,128)(2,1)} %get-tuple-element.48.home_ref), channel_id=1, source_target_pairs={{1,4},{3,6},{4,1},{6,3},{9,12},{11,14},{12,9},{14,11},{17,20},{19,... | collective-permute-start | bytes 3538952 | tf_op jit(solution)/shard_map/ppermute | solution.py:331
  176.6 9.3 %collective-permute-done.8.new_ref = bf16[1,1152,512]{2,1,0:T(8,128)(2,1)S(1)} collective-permute-done((bf16[1,1152,512]{2,1,0:T(8,128)(2,1)}, bf16[1,1152,512]{2,1,0:T(8,128)(2,1)S(1)}, u32[]{:S(2)}, u32[]{:S(2)}) %collective-permute-start.8) | collective-permute-done | bytes 1179680 | tf_op jit(solution)/shard_map/ppermute | solution.py:331
  185.9 1.3 copy-done.5
  187.2 2.5 %shard_map.163 = f32[1,1152,512]{2,1,0:T(8,128)} custom-call(s32[2]{0:T(128)S(1)} %copy-done.12, bf16[1,1152,512]{2,1,0:T(8,128)(2,1)S(1)} %copy-done.5, bf16[1,1152,512]{2,1,0:T(8,128)(2,1)S(1)} %collective-permute-done.8.new_ref), custom_call_target="tpu_custom_call" | custom-call | flops 589824 | bytes 3538944 | tf_op jit(solution)/shard_map/pallas_call | solution.py:444
  189.7 0.0 copy-done.2
  189.7 0.7 shard_map.165
  190.4 0.7 shard_map.166
  191.1 1.6 pad_maximum_fusion
  192.7 0.0 all-to-all-done.3
  192.7 5.0 %shard_map.161 = (bf16[128,1152]{1,0:T(8,128)(2,1)}, bf16[128,1152]{1,0:T(8,128)(2,1)}) custom-call(bf16[16,2,4,8,1152]{4,3,2,1,0:T(8,128)(2,1)} %bitcast.17.back_ref, s32[2,128]{1,0:T(2,128)} %bitcast.28, f32[128,2]{1,0:T(8,128)} %copy-done.10, bf16[128,1152]{1,0:T(8,128)(2,1)} %bitcast.25, bf16[128,1152]{1,0:T(8,128)(2,1)} %copy-done.8, ...), custom_call_target="tpu_custom_call" | custom-call | flops 452984832 | bytes 4718592 | tf_op jit(solution)/shard_map/pallas_call | solution.py:463
  197.7 0.9 collective-permute-done.7.new_ref
  198.6 2.5 %shard_map.164 = f32[1,1152,512]{2,1,0:T(8,128)} custom-call(s32[2]{0:T(128)S(1)} %copy-done.12, bf16[1,1152,512]{2,1,0:T(8,128)(2,1)S(1)} %copy-done.4, bf16[1,1152,512]{2,1,0:T(8,128)(2,1)S(1)} %collective-permute-done.7.new_ref), custom_call_target="tpu_custom_call" | custom-call | flops 589824 | bytes 3538944 | tf_op jit(solution)/shard_map/pallas_call | solution.py:444
  (15 shorter events, 0.0 us)
Async XLA Ops:
  4.0 32.9 %copy-start.17 = (f32[1152]{0:T(1024)S(1)}, f32[1152]{0:T(1024)}, u32[]{:S(2)}) copy-start(f32[1152]{0:T(1024)} %param.17) | copy-start | bytes 13828
  4.0 32.9 %copy-start.16 = (bf16[1152,64]{0,1:T(8,128)(2,1)S(1)}, bf16[1152,64]{0,1:T(8,128)(2,1)}, u32[]{:S(2)}) copy-start(bf16[1152,64]{0,1:T(8,128)(2,1)} %param.18) | copy-start | bytes 442372
  4.0 42.5 %copy-start = (bf16[1152,1152]{1,0:T(8,128)(2,1)S(1)}, bf16[1152,1152]{1,0:T(8,128)(2,1)}, u32[]{:S(2)}) copy-start(bf16[1152,1152]{1,0:T(8,128)(2,1)} %w_out_ref.1) | copy-start | bytes 7962628
  4.0 42.5 %copy-start.13 = (s32[1,1,128,2]{2,3,1,0:T(2,128)S(1)}, s32[1,1,128,2]{2,3,1,0:T(2,128)}, u32[]{:S(2)}) copy-start(s32[1,1,128,2]{2,3,1,0:T(2,128)} %param.19) | copy-start | bytes 3076
  4.0 25.4 %all-to-all-start = ((bf16[32,24,640]{2,1,0:T(8,128)(2,1)}), bf16[32,24,640]{2,1,0:T(8,128)(2,1)}, u32[]{:S(2)}, u32[]{:S(2)}) async-start(bf16[32,24,640]{2,1,0:T(8,128)(2,1)} %bitcast.30), calls=%async_computation | async-start | bytes 1966080 | tf_op jit(solution)/shard_map/all_to_all | solution.py:293
  12.9 37.3 %collective-permute-start = (bf16[1,1152,512]{2,1,0:T(8,128)(2,1)}, bf16[1,1152,512]{2,1,0:T(8,128)(2,1)}, u32[]{:S(2)}, u32[]{:S(2)}) collective-permute-start(bf16[1,1152,512]{2,1,0:T(8,128)(2,1)} %home_gate_ref.1), channel_id=1, source_target_pairs={{1,4},{3,6},{4,1},{6,3},{9,12},{11,14},{12,9},{14,11},{17,20},{19,... | collective-permute-start | bytes 3538952 | tf_op jit(solution)/shard_map/ppermute | solution.py:331
  16.7 33.5 %collective-permute-start.1 = (bf16[1,1152,512]{2,1,0:T(8,128)(2,1)}, bf16[1,1152,512]{2,1,0:T(8,128)(2,1)}, u32[]{:S(2)}, u32[]{:S(2)}) collective-permute-start(bf16[1,1152,512]{2,1,0:T(8,128)(2,1)} %home_up_ref.1), channel_id=1, source_target_pairs={{1,4},{3,6},{4,1},{6,3},{9,12},{11,14},{12,9},{14,11},{17,20},{19,... | collective-permute-start | bytes 3538952 | tf_op jit(solution)/shard_map/ppermute | solution.py:331
  18.6 37.5 %collective-permute-start.2 = (bf16[1,512,1152]{2,1,0:T(8,128)(2,1)}, bf16[1,512,1152]{2,1,0:T(8,128)(2,1)}, u32[]{:S(2)}, u32[]{:S(2)}) collective-permute-start(bf16[1,512,1152]{2,1,0:T(8,128)(2,1)} %home_down_ref.1), channel_id=1, source_target_pairs={{1,4},{3,6},{4,1},{6,3},{9,12},{11,14},{12,9},{14,11},{17,20},{19,... | collective-permute-start | bytes 3538952 | tf_op jit(solution)/shard_map/ppermute | solution.py:331
  32.2 0.7 copy-start.7
  33.0 13.6 %all-to-all-start.1 = ((bf16[32,8,640]{2,1,0:T(8,128)(2,1)}), bf16[32,8,640]{2,1,0:T(8,128)(2,1)S(1)}, u32[]{:S(2)}, u32[]{:S(2)}) async-start(bf16[32,8,640]{2,1,0:T(8,128)(2,1)} %copy-done.7), calls=%async_computation.1 | async-start | bytes 655360 | tf_op jit(solution)/shard_map/all_to_all | solution.py:293
  36.9 62.6 %copy-start.11 = (f32[1,1152]{1,0:T(1,128)}, f32[1,1152]{1,0:T(1,128)S(1)}, u32[]{:S(2)}) copy-start(f32[1,1152]{1,0:T(1,128)S(1)} %reshape.75.gain_ref) | copy-start | bytes 13828
  37.2 62.3 %copy-start.1 = (bf16[1152,64]{1,0:T(8,128)(2,1)}, bf16[1152,64]{1,0:T(8,128)(2,1)S(1)}, u32[]{:S(2)}) copy-start(bf16[1152,64]{1,0:T(8,128)(2,1)S(1)} %copy.17.w_router_ref) | copy-start | bytes 442372
  46.5 1.0 copy-start.6
  47.5 1.0 copy-start.9
  50.2 49.3 %copy-start.8 = (bf16[128,1152]{1,0:T(8,128)(2,1)}, bf16[128,1152]{1,0:T(8,128)(2,1)S(1)}, u32[]{:S(2)}) copy-start(bf16[128,1152]{1,0:T(8,128)(2,1)S(1)} %get-tuple-element.42.hidden_ref) | copy-start | bytes 884740
  50.2 49.3 %copy-start.10 = (f32[128,2]{1,0:T(8,128)}, f32[128,2]{1,0:T(8,128)S(1)}, u32[]{:S(2)}) copy-start(f32[128,2]{1,0:T(8,128)S(1)} %get-tuple-element.41.combine_ref) | copy-start | bytes 3076
  99.5 4.9 %copy-start.15 = (bf16[128,8,1152]{2,1,0:T(8,128)(2,1)}, bf16[128,8,1152]{2,1,0:T(8,128)(2,1)S(1)}, u32[]{:S(2)}) copy-start(bf16[128,8,1152]{2,1,0:T(8,128)(2,1)S(1)} %all_to_all.20) | copy-start | bytes 7077892
  99.5 4.9 %collective-permute-start.3 = (bf16[128,8,1152]{2,1,0:T(8,128)(2,1)S(1)}, bf16[128,8,1152]{2,1,0:T(8,128)(2,1)}, u32[]{:S(2)}, u32[]{:S(2)}) collective-permute-start(bf16[128,8,1152]{2,1,0:T(8,128)(2,1)S(1)} %all_to_all.20), channel_id=1, source_target_pairs={{0,4},{4,0},{8,12},{12,8},{16,20},{20,16},{24,28},{28,24},{32,36},... | collective-permute-start | bytes 7077896 | tf_op jit(solution)/shard_map/ppermute | solution.py:332
  120.5 10.2 %collective-permute-start.4 = (bf16[1024,1152]{1,0:T(8,128)(2,1)}, bf16[1024,1152]{1,0:T(8,128)(2,1)}, u32[]{:S(2)}, u32[]{:S(2)}) collective-permute-start(bf16[1024,1152]{1,0:T(8,128)(2,1)} %get-tuple-element.36), channel_id=1, source_target_pairs={{0,4},{4,0},{8,12},{12,8},{16,20},{20,16},{24,28},{28,24},{32,36},... | collective-permute-start | bytes 7077896 | tf_op jit(solution)/shard_map/ppermute | solution.py:332
  124.4 6.3 %copy-start.14 = (bf16[1024,1152]{1,0:T(8,128)(2,1)S(1)}, bf16[1024,1152]{1,0:T(8,128)(2,1)}, u32[]{:S(2)}) copy-start(bf16[1024,1152]{1,0:T(8,128)(2,1)} %get-tuple-element.35) | copy-start | bytes 7077892
  124.4 11.5 %collective-permute-start.5 = (bf16[1,256,1152]{2,1,0:T(8,128)(2,1)}, bf16[1,256,1152]{2,1,0:T(8,128)(2,1)S(1)}, u32[]{:S(2)}, u32[]{:S(2)}) collective-permute-start(bf16[1,256,1152]{2,1,0:T(8,128)(2,1)} %shard_map.160.home_ref), channel_id=1, source_target_pairs={{1,4},{3,6},{4,1},{6,3},{9,12},{11,14},{12,9},{14,11},{17,20},{19,... | collective-permute-start | bytes 1769480 | tf_op jit(solution)/shard_map/ppermute | solution.py:331
  136.0 4.8 %copy-start.3 = (bf16[1,256,1152]{2,1,0:T(8,128)(2,1)S(1)}, bf16[1,256,1152]{2,1,0:T(8,128)(2,1)}, u32[]{:S(2)}) copy-start(bf16[1,256,1152]{2,1,0:T(8,128)(2,1)} %shard_map.159.home_ref) | copy-start | bytes 1769476
  136.0 56.7 %all-to-all-start.3 = ((bf16[128,8,1152]{2,1,0:T(8,128)(2,1)}), bf16[128,8,1152]{2,1,0:T(8,128)(2,1)}, u32[]{:S(2)}, u32[]{:S(2)}) async-start(bf16[128,8,1152]{2,1,0:T(8,128)(2,1)} %bitcast.16), calls=%async_computation.3 | async-start | bytes 4718592 | tf_op jit(solution)/shard_map/all_to_all | solution.py:293
  140.8 32.5 %collective-permute-start.6 = (bf16[1,256,1152]{2,1,0:T(8,128)(2,1)S(1)}, bf16[1,256,1152]{2,1,0:T(8,128)(2,1)S(1)}, u32[]{:S(2)}, u32[]{:S(2)}) collective-permute-start(bf16[1,256,1152]{2,1,0:T(8,128)(2,1)S(1)} %copy-done.3), channel_id=1, source_target_pairs={{1,4},{3,6},{4,1},{6,3},{9,12},{11,14},{12,9},{14,11},{17,20},{19,... | collective-permute-start | bytes 1769480 | tf_op jit(solution)/shard_map/ppermute | solution.py:331
  143.8 42.1 %copy-start.12 = (s32[2]{0:T(128)S(1)}, s32[2]{0:T(128)}, u32[]{:S(2)}) copy-start(s32[2]{0:T(128)} %pad_add_fusion.state_ref) | copy-start | bytes 28
  150.9 35.0 %collective-permute-start.8 = (bf16[1,1152,512]{2,1,0:T(8,128)(2,1)}, bf16[1,1152,512]{2,1,0:T(8,128)(2,1)S(1)}, u32[]{:S(2)}, u32[]{:S(2)}) collective-permute-start(bf16[1,1152,512]{2,1,0:T(8,128)(2,1)} %get-tuple-element.51.home_ref), channel_id=1, source_target_pairs={{1,4},{3,6},{4,1},{6,3},{9,12},{11,14},{12,9},{14,11},{17,20},{19,... | collective-permute-start | bytes 3538952 | tf_op jit(solution)/shard_map/ppermute | solution.py:331
  173.3 16.4 %copy-start.2 = (bf16[1,256,1152]{2,1,0:T(8,128)(2,1)S(1)}, bf16[1,256,1152]{2,1,0:T(8,128)(2,1)}, u32[]{:S(2)}) copy-start(bf16[1,256,1152]{2,1,0:T(8,128)(2,1)} %shard_map.160.home_ref) | copy-start | bytes 1769476
  173.3 25.3 %collective-permute-start.7 = (bf16[1,1152,512]{2,1,0:T(8,128)(2,1)}, bf16[1,1152,512]{2,1,0:T(8,128)(2,1)S(1)}, u32[]{:S(2)}, u32[]{:S(2)}) collective-permute-start(bf16[1,1152,512]{2,1,0:T(8,128)(2,1)} %get-tuple-element.48.home_ref), channel_id=1, source_target_pairs={{1,4},{3,6},{4,1},{6,3},{9,12},{11,14},{12,9},{14,11},{17,20},{19,... | collective-permute-start | bytes 3538952 | tf_op jit(solution)/shard_map/ppermute | solution.py:331
  185.9 1.3 copy-start.5
  192.7 5.9 %copy-start.4 = (bf16[1,1152,512]{2,1,0:T(8,128)(2,1)S(1)}, bf16[1,1152,512]{2,1,0:T(8,128)(2,1)}, u32[]{:S(2)}) copy-start(bf16[1,1152,512]{2,1,0:T(8,128)(2,1)} %get-tuple-element.48.home_ref) | copy-start | bytes 3538948

commit v4 on v3

--- a/solution.py
+++ b/solution.py
@@ -439,14 +439,14 @@
 
     def widen(home, new):
         _, height, across = home.shape
-        part = height // 4
+        part = height // 8
         pick = lambda n: lambda i, state: (0, jnp.where(state[1] == n, i, 0), 0)
         return pl.pallas_call(
             widen_body,
             out_shape=shape(home.shape, F32),
             grid_spec=pltpu.PrefetchScalarGridSpec(
                 num_scalar_prefetch=1,
-                grid=(4,),
+                grid=(8,),
                 in_specs=[pl.BlockSpec((1, part, across), pick(n)) for n in range(2)],
                 out_specs=pl.BlockSpec((1, part, across), lambda i, state: (0, i, 0)),
             ),

time: 202 us -> 204 us (level)
  Pallas kernels: 49.5 us -> 51.9 us
    pallas_call x4, Pallas kernels: 6.4 us -> 8.82 us  [widen(): pl.pallas_call(widen_body, out_shape=shape(home.shape, F32), grid_spec=pl...]
  transfers between devices with their start and end apart: 12 -> 12, of which waited for: 8 -> 7; matrix products, arithmetic and copies ran while one was open for 3% -> 3% of each run, Pallas kernels for 14% -> 14%
where the time goes in v4:
time: 204 us; the launch traced here: 203 us
  waiting for transfers between devices  56.1 us (28%)
  Pallas kernels  51.9 us (25%)
  blocking collectives  43.3 us (21%)
  starting transfers between devices  39.6 us (19%)
  other arithmetic  6.5 us (3%)
  local copies, waits for them, and re-layouts  4.21 us (2%)
    all_to_all x1, blocking collectives, relay(): return lax.all_to_all(parcel, axes, split_axis=0, concat_axis=0, tiled=True)  43.3 us
    ppermute x7, waiting for transfers between devices, on_device(): swap = lambda a: lax.ppermute(a, everyone, swaps)  36.4 us
    ppermute x7, starting transfers between devices, on_device(): swap = lambda a: lax.ppermute(a, everyone, swaps)  21.1 us
    all_to_all x3, starting transfers between devices, relay(): return lax.all_to_all(parcel, axes, split_axis=0, concat_axis=0, tiled=True)  17.6 us
    all_to_all x3, waiting for transfers between devices, relay(): return lax.all_to_all(parcel, axes, split_axis=0, concat_axis=0, tiled=True)  16.5 us
    pallas_call x1, Pallas kernels, on_device(): call(expert_body, (wide, wide, wide, inner, inner, inner), (6 * product,...  16.1 us
    pallas_call x4, Pallas kernels, widen(): pl.pallas_call(widen_body, out_shape=shape(home.shape, F32), grid_spec=pl...  8.82 us
    pallas_call x2, Pallas kernels, down_rows(): call(down_body, shape((1, half, width), BF16), (product // 2, 2 * total *...  7.14 us
  transfers between devices with their start and end apart: 12, of which 7 were waited for; matrix products, arithmetic and copies ran while one was open for 3% of the time, Pallas kernels for 14%

profile of v4, /device:TPU:1, one launch (start us, length us, event | category | flops | bytes accessed | tf_op | source)
XLA Modules:
  0.0 202.6 jit_solution(17826690483802683727)
XLA Ops:
  0.6 3.4 %shard_map.155 = bf16[16,2,24,640]{3,2,1,0:T(8,128)(2,1)} custom-call(bf16[16,8,1152]{2,1,0:T(8,128)(2,1)} %bitcast.33, bf16[16,8,1152]{2,1,0:T(8,128)(2,1)} %bitcast.34, bf16[16,8,1152]{2,1,0:T(8,128)(2,1)} %bitcast.35), custom_call_target="tpu_custom_call" | custom-call | bytes 1966080 | tf_op jit(solution)/shard_map/pallas_call | solution.py:336
  4.0 0.0 copy-start.13
  4.0 8.9 %all-to-all-start = ((bf16[32,24,640]{2,1,0:T(8,128)(2,1)}), bf16[32,24,640]{2,1,0:T(8,128)(2,1)}, u32[]{:S(2)}, u32[]{:S(2)}) async-start(bf16[32,24,640]{2,1,0:T(8,128)(2,1)} %bitcast.30), calls=%async_computation | async-start | bytes 1966080 | tf_op jit(solution)/shard_map/all_to_all | solution.py:293
  12.9 3.7 %collective-permute-start = (bf16[1,1152,512]{2,1,0:T(8,128)(2,1)}, bf16[1,1152,512]{2,1,0:T(8,128)(2,1)}, u32[]{:S(2)}, u32[]{:S(2)}) collective-permute-start(bf16[1,1152,512]{2,1,0:T(8,128)(2,1)} %home_gate_ref.1), channel_id=1, source_target_pairs={{1,4},{3,6},{4,1},{6,3},{9,12},{11,14},{12,9},{14,11},{17,20},{19,... | collective-permute-start | bytes 3538952 | tf_op jit(solution)/shard_map/ppermute | solution.py:331
  16.7 1.9 collective-permute-start.1
  18.6 3.6 %collective-permute-start.2 = (bf16[1,512,1152]{2,1,0:T(8,128)(2,1)}, bf16[1,512,1152]{2,1,0:T(8,128)(2,1)}, u32[]{:S(2)}, u32[]{:S(2)}) collective-permute-start(bf16[1,512,1152]{2,1,0:T(8,128)(2,1)} %home_down_ref.1), channel_id=1, source_target_pairs={{1,4},{3,6},{4,1},{6,3},{9,12},{11,14},{12,9},{14,11},{17,20},{19,... | collective-permute-start | bytes 3538952 | tf_op jit(solution)/shard_map/ppermute | solution.py:331
  22.3 7.2 %all-to-all-done.refs_1_ = bf16[32,24,640]{2,1,0:T(8,128)(2,1)} async-done(((bf16[32,24,640]{2,1,0:T(8,128)(2,1)}), bf16[32,24,640]{2,1,0:T(8,128)(2,1)}, u32[]{:S(2)}, u32[]{:S(2)}) %all-to-all-start) | async-done | bytes 983072 | tf_op jit(solution)/shard_map/all_to_all | solution.py:293
  29.5 2.8 %shard_map.156 = bf16[32,8,640]{2,1,0:T(8,128)(2,1)S(1)} custom-call(s32[1]{0:T(128)} %bitcast.2.refs_0_, bf16[32,24,640]{2,1,0:T(8,128)(2,1)} %all-to-all-done.refs_1_), custom_call_target="tpu_custom_call" | custom-call | flops 536870912 | bytes 1310720 | tf_op jit(solution)/shard_map/pallas_call | solution.py:346
  32.2 0.0 copy-start.7
  32.2 0.7 copy-done.7
  33.0 3.9 %all-to-all-start.1 = ((bf16[32,8,640]{2,1,0:T(8,128)(2,1)}), bf16[32,8,640]{2,1,0:T(8,128)(2,1)S(1)}, u32[]{:S(2)}, u32[]{:S(2)}) async-start(bf16[32,8,640]{2,1,0:T(8,128)(2,1)} %copy-done.7), calls=%async_computation.1 | async-start | bytes 655360 | tf_op jit(solution)/shard_map/all_to_all | solution.py:293
  36.9 0.0 copy-done.17
  36.9 0.0 copy-done.16
  36.9 0.0 copy-start.11
  36.9 0.2 copy.17.w_router_ref
  37.2 0.0 copy-start.1
  37.2 9.4 %all-to-all-done.1 = bf16[32,8,640]{2,1,0:T(8,128)(2,1)S(1)} async-done(((bf16[32,8,640]{2,1,0:T(8,128)(2,1)}), bf16[32,8,640]{2,1,0:T(8,128)(2,1)S(1)}, u32[]{:S(2)}, u32[]{:S(2)}) %all-to-all-start.1) | async-done | bytes 327712 | tf_op jit(solution)/shard_map/all_to_all | solution.py:293
  46.5 0.0 copy-done
  46.5 0.0 copy-done.13
  46.5 1.0 copy-done.6
  47.5 1.0 copy-done.9
  48.5 1.7 shard_map.157
  50.2 0.0 copy-start.8
  50.2 0.0 copy-start.10
  50.2 0.0 collective-permute-done.new_gate_ref
  50.2 0.0 collective-permute-done.1.new_up_ref
  50.2 5.9 %collective-permute-done.2.new_down_ref = bf16[1,512,1152]{2,1,0:T(8,128)(2,1)} collective-permute-done((bf16[1,512,1152]{2,1,0:T(8,128)(2,1)}, bf16[1,512,1152]{2,1,0:T(8,128)(2,1)}, u32[]{:S(2)}, u32[]{:S(2)}) %collective-permute-start.2) | collective-permute-done | bytes 1179680 | tf_op jit(solution)/shard_map/ppermute | solution.py:331
  56.2 43.3 %all_to_all.20 = bf16[128,8,1152]{2,1,0:T(8,128)(2,1)S(1)} all-to-all(bf16[128,8,1152]{2,1,0:T(8,128)(2,1)S(1)} %bitcast.23), channel_id=1, replica_groups=mesh['frames'=32,'expert'=4] {'frames','expert'}, dimensions={0} | all-to-all | bytes 4718592 | tf_op jit(solution)/shard_map/all_to_all | solution.py:293
  99.5 0.0 copy-done.11
  99.5 0.0 copy-done.1
  99.5 0.0 copy-done.8
  99.5 0.0 copy-done.10
  99.5 0.0 copy-start.15
  99.5 0.6 collective-permute-start.3
  100.1 0.7 pad_add_fusion.state_ref
  100.8 0.6 bitcast_convert_fusion.column_ref
  101.4 3.1 %collective-permute-done.3 = bf16[128,8,1152]{2,1,0:T(8,128)(2,1)} collective-permute-done((bf16[128,8,1152]{2,1,0:T(8,128)(2,1)S(1)}, bf16[128,8,1152]{2,1,0:T(8,128)(2,1)}, u32[]{:S(2)}, u32[]{:S(2)}) %collective-permute-start.3) | collective-permute-done | bytes 2359328 | tf_op jit(solution)/shard_map/ppermute | solution.py:332
  104.5 0.0 copy-done.15
  104.5 16.1 %shard_map.158 = (bf16[1024,1152]{1,0:T(8,128)(2,1)}, bf16[1024,1152]{1,0:T(8,128)(2,1)}, bf16[1024,1152]{1,0:T(8,128)(2,1)}, bf16[1024,512]{1,0:T(8,128)(2,1)},...) custom-call(s32[2]{0:T(128)} %pad_add_fusion.state_ref, bf16[1024,1152]{1,0:T(8,128)(2,1)} %bitcast.31, ...), custom_call_target="tpu_custom_call" | custom-call | flops 7247757312 | bytes 23592960 | tf_op jit(solution)/shard_map/pallas_call | solution.py:377
  120.5 0.4 collective-permute-start.4
  120.9 3.5 %shard_map.160.home_ref = bf16[1,256,1152]{2,1,0:T(8,128)(2,1)} custom-call(bf16[1024,512]{1,0:T(8,128)(2,1)} %get-tuple-element.37.units_ref, bf16[1024,1152]{1,0:T(8,128)(2,1)} %get-tuple-element.38.scaled_ref), custom_call_target="tpu_custom_call" | custom-call | flops 603979776 | bytes 4718592 | tf_op jit(solution)/shard_map/pallas_call | solution.py:397
  124.4 2.7 %collective-permute-start.5 = (bf16[1,256,1152]{2,1,0:T(8,128)(2,1)}, bf16[1,256,1152]{2,1,0:T(8,128)(2,1)S(1)}, u32[]{:S(2)}, u32[]{:S(2)}) collective-permute-start(bf16[1,256,1152]{2,1,0:T(8,128)(2,1)} %shard_map.160.home_ref), channel_id=1, source_target_pairs={{1,4},{3,6},{4,1},{6,3},{9,12},{11,14},{12,9},{14,11},{17,20},{19,... | collective-permute-start | bytes 1769480 | tf_op jit(solution)/shard_map/ppermute | solution.py:331
  127.1 3.6 %shard_map.159.home_ref = bf16[1,256,1152]{2,1,0:T(8,128)(2,1)} custom-call(bf16[1024,512]{1,0:T(8,128)(2,1)} %get-tuple-element.37.units_ref, bf16[1024,1152]{1,0:T(8,128)(2,1)} %get-tuple-element.38.scaled_ref), custom_call_target="tpu_custom_call" | custom-call | flops 603979776 | bytes 4718592 | tf_op jit(solution)/shard_map/pallas_call | solution.py:397
  130.7 0.0 collective-permute-done.4
  130.7 0.0 copy-done.14
  130.7 3.6 %add_convert_fusion = bf16[1024,1152]{1,0:T(8,128)(2,1)} fusion(bf16[1024,1152]{1,0:T(8,128)(2,1)} %collective-permute-done.4, bf16[1024,1152]{1,0:T(8,128)(2,1)S(1)} %copy-done.14), kind=kLoop, calls=%fused_computation | loop fusion | flops 4718592 | bytes 7077888 | tf_op jit(solution)/shard_map/convert_element_type | solution.py:411
  134.4 1.6 collective-permute-done.5.new_ref
  136.0 4.8 %all-to-all-start.3 = ((bf16[128,8,1152]{2,1,0:T(8,128)(2,1)}), bf16[128,8,1152]{2,1,0:T(8,128)(2,1)}, u32[]{:S(2)}, u32[]{:S(2)}) async-start(bf16[128,8,1152]{2,1,0:T(8,128)(2,1)} %bitcast.16), calls=%async_computation.3 | async-start | bytes 4718592 | tf_op jit(solution)/shard_map/all_to_all | solution.py:293
  140.8 0.0 copy-done.3
  140.8 3.0 %collective-permute-start.6 = (bf16[1,256,1152]{2,1,0:T(8,128)(2,1)S(1)}, bf16[1,256,1152]{2,1,0:T(8,128)(2,1)S(1)}, u32[]{:S(2)}, u32[]{:S(2)}) collective-permute-start(bf16[1,256,1152]{2,1,0:T(8,128)(2,1)S(1)} %copy-done.3), channel_id=1, source_target_pairs={{1,4},{3,6},{4,1},{6,3},{9,12},{11,14},{12,9},{14,11},{17,20},{19,... | collective-permute-start | bytes 1769480 | tf_op jit(solution)/shard_map/ppermute | solution.py:331
  143.8 7.1 %shard_map.162 = (bf16[1,1152,512]{2,1,0:T(8,128)(2,1)}, bf16[1,1152,512]{2,1,0:T(8,128)(2,1)}) custom-call(s32[2]{0:T(128)} %pad_add_fusion.state_ref, bf16[1024,1152]{1,0:T(8,128)(2,1)} %bitcast.32, bf16[1024,1152]{1,0:T(8,128)(2,1)} %bitcast.14.there_ref, bf16[1024,512]{1,0:T(8,128)(2,1)} %get-tuple-element.44.left_ref, ...), custom_call_target="tpu_custom_call" | custom-call | flops 2415919104 | bytes 9437184 | tf_op jit(solution)/shard_map/pallas_call | solution.py:420
  150.9 2.8 %collective-permute-start.8 = (bf16[1,1152,512]{2,1,0:T(8,128)(2,1)}, bf16[1,1152,512]{2,1,0:T(8,128)(2,1)S(1)}, u32[]{:S(2)}, u32[]{:S(2)}) collective-permute-start(bf16[1,1152,512]{2,1,0:T(8,128)(2,1)} %get-tuple-element.51.home_ref), channel_id=1, source_target_pairs={{1,4},{3,6},{4,1},{6,3},{9,12},{11,14},{12,9},{14,11},{17,20},{19,... | collective-permute-start | bytes 3538952 | tf_op jit(solution)/shard_map/ppermute | solution.py:331
  153.7 19.6 %collective-permute-done.6.new_ref = bf16[1,256,1152]{2,1,0:T(8,128)(2,1)S(1)} collective-permute-done((bf16[1,256,1152]{2,1,0:T(8,128)(2,1)S(1)}, bf16[1,256,1152]{2,1,0:T(8,128)(2,1)S(1)}, u32[]{:S(2)}, u32[]{:S(2)}) %collective-permute-start.6) | collective-permute-done | bytes 589856 | tf_op jit(solution)/shard_map/ppermute | solution.py:331
  173.3 3.3 %collective-permute-start.7 = (bf16[1,1152,512]{2,1,0:T(8,128)(2,1)}, bf16[1,1152,512]{2,1,0:T(8,128)(2,1)S(1)}, u32[]{:S(2)}, u32[]{:S(2)}) collective-permute-start(bf16[1,1152,512]{2,1,0:T(8,128)(2,1)} %get-tuple-element.48.home_ref), channel_id=1, source_target_pairs={{1,4},{3,6},{4,1},{6,3},{9,12},{11,14},{12,9},{14,11},{17,20},{19,... | collective-permute-start | bytes 3538952 | tf_op jit(solution)/shard_map/ppermute | solution.py:331
  176.6 9.3 %collective-permute-done.8.new_ref = bf16[1,1152,512]{2,1,0:T(8,128)(2,1)S(1)} collective-permute-done((bf16[1,1152,512]{2,1,0:T(8,128)(2,1)}, bf16[1,1152,512]{2,1,0:T(8,128)(2,1)S(1)}, u32[]{:S(2)}, u32[]{:S(2)}) %collective-permute-start.8) | collective-permute-done | bytes 1179680 | tf_op jit(solution)/shard_map/ppermute | solution.py:331
  185.9 1.3 copy-done.5
  187.2 3.6 %shard_map.163 = f32[1,1152,512]{2,1,0:T(8,128)} custom-call(s32[2]{0:T(128)S(1)} %copy-done.12, bf16[1,1152,512]{2,1,0:T(8,128)(2,1)S(1)} %copy-done.5, bf16[1,1152,512]{2,1,0:T(8,128)(2,1)S(1)} %collective-permute-done.8.new_ref), custom_call_target="tpu_custom_call" | custom-call | flops 589824 | bytes 3538944 | tf_op jit(solution)/shard_map/pallas_call | solution.py:444
  190.8 0.8 shard_map.165
  191.6 0.8 shard_map.166
  192.4 1.6 pad_maximum_fusion
  194.0 0.0 all-to-all-done.3
  194.0 5.0 %shard_map.161 = (bf16[128,1152]{1,0:T(8,128)(2,1)}, bf16[128,1152]{1,0:T(8,128)(2,1)}) custom-call(bf16[16,2,4,8,1152]{4,3,2,1,0:T(8,128)(2,1)} %bitcast.17.back_ref, s32[2,128]{1,0:T(2,128)} %bitcast.28, f32[128,2]{1,0:T(8,128)} %copy-done.10, bf16[128,1152]{1,0:T(8,128)(2,1)} %bitcast.25, bf16[128,1152]{1,0:T(8,128)(2,1)} %copy-done.8, ...), custom_call_target="tpu_custom_call" | custom-call | flops 452984832 | bytes 4718592 | tf_op jit(solution)/shard_map/pallas_call | solution.py:463
  199.0 0.0 collective-permute-done.7.new_ref
  199.0 3.6 %shard_map.164 = f32[1,1152,512]{2,1,0:T(8,128)} custom-call(s32[2]{0:T(128)S(1)} %copy-done.12, bf16[1,1152,512]{2,1,0:T(8,128)(2,1)S(1)} %copy-done.4, bf16[1,1152,512]{2,1,0:T(8,128)(2,1)S(1)} %collective-permute-done.7.new_ref), custom_call_target="tpu_custom_call" | custom-call | flops 589824 | bytes 3538944 | tf_op jit(solution)/shard_map/pallas_call | solution.py:444
  (15 shorter events, 0.0 us)
Async XLA Ops:
  4.0 32.9 %copy-start.17 = (f32[1152]{0:T(1024)S(1)}, f32[1152]{0:T(1024)}, u32[]{:S(2)}) copy-start(f32[1152]{0:T(1024)} %param.17) | copy-start | bytes 13828
  4.0 32.9 %copy-start.16 = (bf16[1152,64]{0,1:T(8,128)(2,1)S(1)}, bf16[1152,64]{0,1:T(8,128)(2,1)}, u32[]{:S(2)}) copy-start(bf16[1152,64]{0,1:T(8,128)(2,1)} %param.18) | copy-start | bytes 442372
  4.0 42.5 %copy-start = (bf16[1152,1152]{1,0:T(8,128)(2,1)S(1)}, bf16[1152,1152]{1,0:T(8,128)(2,1)}, u32[]{:S(2)}) copy-start(bf16[1152,1152]{1,0:T(8,128)(2,1)} %w_out_ref.1) | copy-start | bytes 7962628
  4.0 42.5 %copy-start.13 = (s32[1,1,128,2]{2,3,1,0:T(2,128)S(1)}, s32[1,1,128,2]{2,3,1,0:T(2,128)}, u32[]{:S(2)}) copy-start(s32[1,1,128,2]{2,3,1,0:T(2,128)} %param.19) | copy-start | bytes 3076
  4.0 25.4 %all-to-all-start = ((bf16[32,24,640]{2,1,0:T(8,128)(2,1)}), bf16[32,24,640]{2,1,0:T(8,128)(2,1)}, u32[]{:S(2)}, u32[]{:S(2)}) async-start(bf16[32,24,640]{2,1,0:T(8,128)(2,1)} %bitcast.30), calls=%async_computation | async-start | bytes 1966080 | tf_op jit(solution)/shard_map/all_to_all | solution.py:293
  12.9 37.3 %collective-permute-start = (bf16[1,1152,512]{2,1,0:T(8,128)(2,1)}, bf16[1,1152,512]{2,1,0:T(8,128)(2,1)}, u32[]{:S(2)}, u32[]{:S(2)}) collective-permute-start(bf16[1,1152,512]{2,1,0:T(8,128)(2,1)} %home_gate_ref.1), channel_id=1, source_target_pairs={{1,4},{3,6},{4,1},{6,3},{9,12},{11,14},{12,9},{14,11},{17,20},{19,... | collective-permute-start | bytes 3538952 | tf_op jit(solution)/shard_map/ppermute | solution.py:331
  16.7 33.5 %collective-permute-start.1 = (bf16[1,1152,512]{2,1,0:T(8,128)(2,1)}, bf16[1,1152,512]{2,1,0:T(8,128)(2,1)}, u32[]{:S(2)}, u32[]{:S(2)}) collective-permute-start(bf16[1,1152,512]{2,1,0:T(8,128)(2,1)} %home_up_ref.1), channel_id=1, source_target_pairs={{1,4},{3,6},{4,1},{6,3},{9,12},{11,14},{12,9},{14,11},{17,20},{19,... | collective-permute-start | bytes 3538952 | tf_op jit(solution)/shard_map/ppermute | solution.py:331
  18.6 37.5 %collective-permute-start.2 = (bf16[1,512,1152]{2,1,0:T(8,128)(2,1)}, bf16[1,512,1152]{2,1,0:T(8,128)(2,1)}, u32[]{:S(2)}, u32[]{:S(2)}) collective-permute-start(bf16[1,512,1152]{2,1,0:T(8,128)(2,1)} %home_down_ref.1), channel_id=1, source_target_pairs={{1,4},{3,6},{4,1},{6,3},{9,12},{11,14},{12,9},{14,11},{17,20},{19,... | collective-permute-start | bytes 3538952 | tf_op jit(solution)/shard_map/ppermute | solution.py:331
  32.2 0.7 copy-start.7
  33.0 13.6 %all-to-all-start.1 = ((bf16[32,8,640]{2,1,0:T(8,128)(2,1)}), bf16[32,8,640]{2,1,0:T(8,128)(2,1)S(1)}, u32[]{:S(2)}, u32[]{:S(2)}) async-start(bf16[32,8,640]{2,1,0:T(8,128)(2,1)} %copy-done.7), calls=%async_computation.1 | async-start | bytes 655360 | tf_op jit(solution)/shard_map/all_to_all | solution.py:293
  36.9 62.6 %copy-start.11 = (f32[1,1152]{1,0:T(1,128)}, f32[1,1152]{1,0:T(1,128)S(1)}, u32[]{:S(2)}) copy-start(f32[1,1152]{1,0:T(1,128)S(1)} %reshape.75.gain_ref) | copy-start | bytes 13828
  37.2 62.3 %copy-start.1 = (bf16[1152,64]{1,0:T(8,128)(2,1)}, bf16[1152,64]{1,0:T(8,128)(2,1)S(1)}, u32[]{:S(2)}) copy-start(bf16[1152,64]{1,0:T(8,128)(2,1)S(1)} %copy.17.w_router_ref) | copy-start | bytes 442372
  46.5 1.0 copy-start.6
  47.5 1.0 copy-start.9
  50.2 49.3 %copy-start.8 = (bf16[128,1152]{1,0:T(8,128)(2,1)}, bf16[128,1152]{1,0:T(8,128)(2,1)S(1)}, u32[]{:S(2)}) copy-start(bf16[128,1152]{1,0:T(8,128)(2,1)S(1)} %get-tuple-element.42.hidden_ref) | copy-start | bytes 884740
  50.2 49.3 %copy-start.10 = (f32[128,2]{1,0:T(8,128)}, f32[128,2]{1,0:T(8,128)S(1)}, u32[]{:S(2)}) copy-start(f32[128,2]{1,0:T(8,128)S(1)} %get-tuple-element.41.combine_ref) | copy-start | bytes 3076
  99.5 4.9 %copy-start.15 = (bf16[128,8,1152]{2,1,0:T(8,128)(2,1)}, bf16[128,8,1152]{2,1,0:T(8,128)(2,1)S(1)}, u32[]{:S(2)}) copy-start(bf16[128,8,1152]{2,1,0:T(8,128)(2,1)S(1)} %all_to_all.20) | copy-start | bytes 7077892
  99.5 4.9 %collective-permute-start.3 = (bf16[128,8,1152]{2,1,0:T(8,128)(2,1)S(1)}, bf16[128,8,1152]{2,1,0:T(8,128)(2,1)}, u32[]{:S(2)}, u32[]{:S(2)}) collective-permute-start(bf16[128,8,1152]{2,1,0:T(8,128)(2,1)S(1)} %all_to_all.20), channel_id=1, source_target_pairs={{0,4},{4,0},{8,12},{12,8},{16,20},{20,16},{24,28},{28,24},{32,36},... | collective-permute-start | bytes 7077896 | tf_op jit(solution)/shard_map/ppermute | solution.py:332
  120.5 10.2 %collective-permute-start.4 = (bf16[1024,1152]{1,0:T(8,128)(2,1)}, bf16[1024,1152]{1,0:T(8,128)(2,1)}, u32[]{:S(2)}, u32[]{:S(2)}) collective-permute-start(bf16[1024,1152]{1,0:T(8,128)(2,1)} %get-tuple-element.36), channel_id=1, source_target_pairs={{0,4},{4,0},{8,12},{12,8},{16,20},{20,16},{24,28},{28,24},{32,36},... | collective-permute-start | bytes 7077896 | tf_op jit(solution)/shard_map/ppermute | solution.py:332
  124.4 6.3 %copy-start.14 = (bf16[1024,1152]{1,0:T(8,128)(2,1)S(1)}, bf16[1024,1152]{1,0:T(8,128)(2,1)}, u32[]{:S(2)}) copy-start(bf16[1024,1152]{1,0:T(8,128)(2,1)} %get-tuple-element.35) | copy-start | bytes 7077892
  124.4 11.5 %collective-permute-start.5 = (bf16[1,256,1152]{2,1,0:T(8,128)(2,1)}, bf16[1,256,1152]{2,1,0:T(8,128)(2,1)S(1)}, u32[]{:S(2)}, u32[]{:S(2)}) collective-permute-start(bf16[1,256,1152]{2,1,0:T(8,128)(2,1)} %shard_map.160.home_ref), channel_id=1, source_target_pairs={{1,4},{3,6},{4,1},{6,3},{9,12},{11,14},{12,9},{14,11},{17,20},{19,... | collective-permute-start | bytes 1769480 | tf_op jit(solution)/shard_map/ppermute | solution.py:331
  136.0 4.8 %copy-start.3 = (bf16[1,256,1152]{2,1,0:T(8,128)(2,1)S(1)}, bf16[1,256,1152]{2,1,0:T(8,128)(2,1)}, u32[]{:S(2)}) copy-start(bf16[1,256,1152]{2,1,0:T(8,128)(2,1)} %shard_map.159.home_ref) | copy-start | bytes 1769476
  136.0 58.0 %all-to-all-start.3 = ((bf16[128,8,1152]{2,1,0:T(8,128)(2,1)}), bf16[128,8,1152]{2,1,0:T(8,128)(2,1)}, u32[]{:S(2)}, u32[]{:S(2)}) async-start(bf16[128,8,1152]{2,1,0:T(8,128)(2,1)} %bitcast.16), calls=%async_computation.3 | async-start | bytes 4718592 | tf_op jit(solution)/shard_map/all_to_all | solution.py:293
  140.8 32.5 %collective-permute-start.6 = (bf16[1,256,1152]{2,1,0:T(8,128)(2,1)S(1)}, bf16[1,256,1152]{2,1,0:T(8,128)(2,1)S(1)}, u32[]{:S(2)}, u32[]{:S(2)}) collective-permute-start(bf16[1,256,1152]{2,1,0:T(8,128)(2,1)S(1)} %copy-done.3), channel_id=1, source_target_pairs={{1,4},{3,6},{4,1},{6,3},{9,12},{11,14},{12,9},{14,11},{17,20},{19,... | collective-permute-start | bytes 1769480 | tf_op jit(solution)/shard_map/ppermute | solution.py:331
  143.8 42.1 %copy-start.12 = (s32[2]{0:T(128)S(1)}, s32[2]{0:T(128)}, u32[]{:S(2)}) copy-start(s32[2]{0:T(128)} %pad_add_fusion.state_ref) | copy-start | bytes 28
  150.9 35.0 %collective-permute-start.8 = (bf16[1,1152,512]{2,1,0:T(8,128)(2,1)}, bf16[1,1152,512]{2,1,0:T(8,128)(2,1)S(1)}, u32[]{:S(2)}, u32[]{:S(2)}) collective-permute-start(bf16[1,1152,512]{2,1,0:T(8,128)(2,1)} %get-tuple-element.51.home_ref), channel_id=1, source_target_pairs={{1,4},{3,6},{4,1},{6,3},{9,12},{11,14},{12,9},{14,11},{17,20},{19,... | collective-permute-start | bytes 3538952 | tf_op jit(solution)/shard_map/ppermute | solution.py:331
  173.3 17.5 %copy-start.2 = (bf16[1,256,1152]{2,1,0:T(8,128)(2,1)S(1)}, bf16[1,256,1152]{2,1,0:T(8,128)(2,1)}, u32[]{:S(2)}) copy-start(bf16[1,256,1152]{2,1,0:T(8,128)(2,1)} %shard_map.160.home_ref) | copy-start | bytes 1769476
  173.3 25.7 %collective-permute-start.7 = (bf16[1,1152,512]{2,1,0:T(8,128)(2,1)}, bf16[1,1152,512]{2,1,0:T(8,128)(2,1)S(1)}, u32[]{:S(2)}, u32[]{:S(2)}) collective-permute-start(bf16[1,1152,512]{2,1,0:T(8,128)(2,1)} %get-tuple-element.48.home_ref), channel_id=1, source_target_pairs={{1,4},{3,6},{4,1},{6,3},{9,12},{11,14},{12,9},{14,11},{17,20},{19,... | collective-permute-start | bytes 3538952 | tf_op jit(solution)/shard_map/ppermute | solution.py:331
  185.9 1.3 copy-start.5
  194.0 5.0 %copy-start.4 = (bf16[1,1152,512]{2,1,0:T(8,128)(2,1)S(1)}, bf16[1,1152,512]{2,1,0:T(8,128)(2,1)}, u32[]{:S(2)}) copy-start(bf16[1,1152,512]{2,1,0:T(8,128)(2,1)} %get-tuple-element.48.home_ref) | copy-start | bytes 3538948
